TPU v7x, 1024 devices: a whole 8x8x8 slice. The times are simulated.
1024 devices in a mesh: mp: 64 (over z, y), dp: 16 (over x, core).
Axes of the slice: x: 8, y: 8, z: 8, core: 2. Of those that a mesh axis runs over, the one named last changes fastest.
Arguments:
- momentum: float32 [8192, 28672], P('mp', 'dp'), may hold values from -120 to 120, as said below
- gradient: bfloat16 [8192, 28672], P('mp', 'dp'), may hold values from -4 to 4
- factor_q: bfloat16 [28672, 128], P(('dp', 'mp')), may hold values from -0.03125 to 0.03125
Outputs:
- momentum_out: float32 [8192, 28672], P('mp', 'dp')
- factor_out: bfloat16 [28672, 128], P(('dp', 'mp'))
- update: bfloat16 [8192, 28672], P('mp', 'dp')
Inputs may be any that keep to these rules, and one draw needn't show every extreme that they name: `momentum`: entries are finite reals.
All inputs are finite; a program needn't handle non-finite values.
Results may differ from a plain program's by a relative error of at most 0.00135.
Values may be sent and summed in bfloat16 or wider, within the bound.
No kernel may reach another device: no remote copies, remote signals or barrier semaphores. Data moves between devices by JAX's collectives and lax.ppermute only.
A program may use at most 32 MiB of HBM per device.

v0:
```python
import math

import jax
import jax.numpy as jnp
from jax import lax
from jax.sharding import PartitionSpec as P

D = 8192
FF = 28672
RANK = 128


highest = lax.Precision.HIGHEST
feedback_rate = 0.05


def make_orthonormal(power_left, gram_matrix):
    factor_low = jnp.linalg.cholesky(gram_matrix)
    return jax.scipy.linalg.solve_triangular(factor_low, power_left.T, lower=True).T


def local(momentum, gradient, factor_q):
    blended = momentum + gradient.astype(jnp.float32)
    cols_local = blended.shape[1]
    share_rows = cols_local // lax.axis_size("mp")
    power_part = jnp.dot(
        blended,
        lax.all_gather(factor_q, "mp", axis=0, tiled=True).astype(jnp.float32),
        precision=highest,
    )
    power_left = lax.psum(power_part, "dp")
    gram_matrix = lax.psum(jnp.dot(power_left.T, power_left, precision=highest), "mp")
    orthonormal = make_orthonormal(power_left, gram_matrix)
    right_part = jnp.dot(blended.T, orthonormal, precision=highest)
    power_right = lax.psum(right_part, "mp")
    column_sums = lax.psum(jnp.sum(power_right * power_right, axis=0), "dp")
    q_new = power_right * lax.rsqrt(column_sums + 1e-06)
    q_share = lax.dynamic_slice_in_dim(q_new, lax.axis_index("mp") * share_rows, share_rows, 0)
    momentum_out = blended - feedback_rate * jnp.dot(orthonormal, power_right.T, precision=highest)
    scale_factor = math.sqrt(D * FF / RANK)
    update = (scale_factor * jnp.dot(orthonormal, q_new.T, precision=highest)).astype(jnp.bfloat16)
    return (momentum_out, q_share.astype(jnp.bfloat16), update)


def solution(mesh):
    return jax.shard_map(
        local,
        mesh=mesh,
        in_specs=(P("mp", "dp"), P("mp", "dp"), P(("dp", "mp"), None)),
        out_specs=(P("mp", "dp"), P(("dp", "mp"), None), P("mp", "dp")),
        check_vma=False,
    )
```

profile of v0, /device:TPU:1, one launch (start us, length us, event | category | flops | bytes accessed | tf_op | source)
XLA Modules:
  0.0 583.0 jit_solution(5538085761111015608)
XLA Ops:
  7.2 0.0 copy-start
  7.2 0.0 all-reduce.4.cloned.1.call-start
  7.2 53.0 %all-gather = bf16[64,28,128]{2,1,0:T(8,128)(2,1)S(1)} all-gather(bf16[1,28,128]{2,1,0:T(8,128)(2,1)} %bitcast.19), channel_id=1, replica_groups=mesh['mp'=64,'dp'=16] {'mp'}, dimensions={0}, use_global_device_ids=true | all-gather | bytes 465920 | tf_op jit(solution)/shard_map/all_gather | solution.py:28
  60.2 0.1 reshape.18
  60.3 0.0 copy-done
  60.3 0.9 copy-done.2
  61.2 1.2 fusion.3
  62.5 0.0 all-reduce.4.cloned.1.call-update
  62.5 0.0 all-reduce.6.cloned.1.call-start
  62.6 120.4 %all-reduce.4.cloned.1.call-done = f32[128,128]{1,0:T(8,128)} async-done(((f32[128,128]{1,0:T(8,128)}), f32[128,128]{1,0:T(8,128)}) %all-reduce.4.cloned.1.call-update) | async-done | bytes 65552 | tf_op jit(solution)/shard_map/psum | solution.py:31
  182.9 1.8 fusion.8
  184.8 0.0 all-reduce.6.cloned.1.call-update
  184.8 0.0 all-reduce.8.cloned.1.call-start
  184.8 160.8 %all-reduce.6.cloned.1.call-done = f32[128,128]{0,1:T(8,128)} async-done(((f32[128,128]{0,1:T(8,128)}), f32[128,128]{0,1:T(8,128)}) %all-reduce.6.cloned.1.call-update) | async-done | bytes 65552 | tf_op jit(solution)/shard_map/psum | solution.py:32
  345.7 1.0 copy.11
  346.7 0.0 copy-done.4
  346.7 11.7 %cholesky.16 = f32[128,128]{1,0:T(8,128)S(1)} custom-call(f32[128,128]{1,0:T(8,128)S(1)} %fusion.7), custom_call_target="Cholesky" | custom-call | tf_op jit(solution)/shard_map/jit(cholesky)/cholesky | solution.py:18
  358.5 0.6 compare_reduce_fusion
  359.1 0.7 fusion.4
  359.8 9.8 %custom-call.7 = f32[1,128,128]{1,2,0:T(8,128)S(1)} custom-call(f32[1,128,128]{2,1,0:T(8,128)S(1)} %fusion.4), custom_call_target="InvertDiagBlocksLowerTriangular" | custom-call | tf_op jit(solution)/shard_map/jit(_solve_triangular)/triangular_solve | solution.py:19
  369.6 0.0 copy-done.3
  369.6 0.3 fusion.5
  369.9 2.5 fusion.2
  372.4 0.0 all-reduce.8.cloned.1.call-update
  372.5 170.3 %all-reduce.8.cloned.1.call-done = f32[1792,128]{1,0:T(8,128)} async-done(((f32[1792,128]{1,0:T(8,128)}), f32[1792,128]{1,0:T(8,128)}) %all-reduce.8.cloned.1.call-update) | async-done | bytes 917520 | tf_op jit(solution)/shard_map/psum | solution.py:35
  542.8 1.5 multiply_reduce_fusion
  544.3 27.8 %psum.31 = f32[128]{0:T(128)S(1)} all-reduce(f32[128]{0:T(128)S(1)} %multiply_reduce_fusion), channel_id=1, replica_groups=mesh['mp'=64,'dp'=16] {'dp'}, use_global_device_ids=true, to_apply=%region_6.7 | all-reduce | flops 128 | bytes 1024 | tf_op jit(solution)/shard_map/psum | solution.py:36
  572.1 0.0 copy-done.1
  572.1 0.1 broadcast_multiply_fusion
  572.2 1.7 fusion.1
  573.9 0.6 dynamic-slice_convert_fusion
  574.5 1.9 fusion
  (7 shorter events, 0.1 us)
Async XLA Ops:
  7.2 53.2 %copy-start = (f32[128,1792]{1,0:T(8,128)S(1)}, f32[128,1792]{1,0:T(8,128)}, u32[]{:S(2)}) copy-start(f32[128,1792]{1,0:T(8,128)} %param.3) | copy-start | bytes 2752516
  7.2 175.8 %all-reduce.4.cloned.1.call-start = ((), (), s32[]{:S(2)}) async-start(), calls=%async_computation | async-start | bytes 131072 | tf_op jit(solution)/shard_map/psum | solution.py:31
  60.2 1.0 copy-start.2
  62.5 283.2 %all-reduce.6.cloned.1.call-start = ((), (), s32[]{:S(2)}) async-start(), calls=%async_computation.1 | async-start | bytes 131072 | tf_op jit(solution)/shard_map/psum | solution.py:32
  184.8 358.0 %all-reduce.8.cloned.1.call-start = ((), (), s32[]{:S(2)}) async-start(), calls=%async_computation.2 | async-start | bytes 1835008 | tf_op jit(solution)/shard_map/psum | solution.py:35
  345.7 1.0 copy-start.4
  359.1 10.5 %copy-start.3 = (f32[128,128]{1,0:T(8,128)S(1)}, f32[128,128]{1,0:T(8,128)}, u32[]{:S(2)}) copy-start(f32[128,128]{1,0:T(8,128)} %all-reduce.4.cloned.1.call-done) | copy-start | bytes 196612
  542.8 29.3 %copy-start.1 = (f32[1792,128]{1,0:T(8,128)S(1)}, f32[1792,128]{1,0:T(8,128)}, u32[]{:S(2)}) copy-start(f32[1792,128]{1,0:T(8,128)} %all-reduce.8.cloned.1.call-done) | copy-start | bytes 2752516
Sparse Core Ops, SparseCore 0:
  62.6 120.2 all-reduce.3
  186.8 158.8 all-reduce.5
  372.6 170.1 all-reduce.7
where the time goes:
time: 583 us
  waiting for transfers between devices  452 us (78%)
  blocking collectives  80.8 us (14%)
  other arithmetic  24.5 us (4%)
  between operations  13.8 us (2%)
  matrix products  9.5 us (2%)
    psum x1, waiting for transfers between devices, local(): power_right = lax.psum(right_part, 'mp')  170 us
    psum x1, waiting for transfers between devices, local(): lax.psum(jnp.dot(power_left.T, power_left, precision=highest), 'mp')  161 us
    psum x1, waiting for transfers between devices, local(): power_left = lax.psum(power_part, 'dp')  120 us
    all_gather x1, blocking collectives, local(): lax.all_gather(factor_q, 'mp', axis=0, tiled=True).astype(jnp.float32)  53 us
    psum x1, blocking collectives, local(): column_sums = lax.psum(jnp.sum(power_right * power_right, axis=0), 'dp')  27.8 us
    another operation x3, other arithmetic, make_orthonormal(): factor_low = jnp.linalg.cholesky(gram_matrix)  12.4 us
  transfers between devices with their start and end apart: 3, of which 3 were waited for; matrix products, arithmetic and copies ran while one was open for 0% of the time, Pallas kernels for 0%

commit v1 on v0

v1 whole, which is shorter than its diff:
```python
import math

import jax
import jax.numpy as jnp
from jax import lax
from jax.sharding import Mesh
from jax.sharding import PartitionSpec as P

D = 8192
FF = 28672
RANK = 128
SIDE = 8
SHARE = 28
SLOT = 32

highest = lax.Precision.HIGHEST
feedback_rate = 0.05


def exchange(blocks, axis):
    return lax.all_to_all(blocks, axis, 0, 0, tiled=False)


def gather_blocks(block, axis, size):
    return exchange(jnp.broadcast_to(block[None], (size, *block.shape)), axis)


def sum_over_dp(part):
    rows = part.shape[0] // 2
    core = lax.axis_index("c")
    kept = lax.dynamic_slice_in_dim(part, core * rows, rows, 0)
    given = lax.dynamic_slice_in_dim(part, (1 - core) * rows, rows, 0)
    half = kept + lax.ppermute(given, "c", [(0, 1), (1, 0)])
    piece = jnp.sum(exchange(half.reshape(SIDE, rows // SIDE, RANK), "x"), axis=0)
    half = gather_blocks(piece, "x", SIDE).reshape(rows, RANK)
    other = lax.ppermute(half, "c", [(0, 1), (1, 0)])
    low = jnp.where(core == 0, half, other)
    high = jnp.where(core == 0, other, half)
    return jnp.concatenate([low, high], axis=0)


def local(momentum, gradient, factor_q):
    blended = momentum + gradient.astype(jnp.float32)
    cols_local = blended.shape[1]
    q_cols = gather_blocks(factor_q, ("z", "y"), SIDE * SIDE).reshape(cols_local, RANK)
    power_left = sum_over_dp(jnp.dot(blended, q_cols.astype(jnp.float32), precision=highest))
    gram_part = jnp.dot(power_left.T, power_left, precision=highest)
    raw_part = jnp.dot(blended.T, power_left, precision=highest)
    payload = jnp.concatenate(
        [
            raw_part.reshape(SIDE, SIDE, SHARE, RANK),
            gram_part.reshape(SIDE, SIDE, 2, RANK),
            jnp.zeros((SIDE, SIDE, SLOT - SHARE - 2, RANK), jnp.float32),
        ],
        axis=2,
    )
    over_z = jnp.sum(exchange(payload, "z"), axis=0)
    slot = jnp.sum(exchange(over_z, "y"), axis=0)
    slots = gather_blocks(gather_blocks(slot, "y", SIDE), "z", SIDE)
    gram_matrix = slots[:, :, SHARE : SHARE + 2].reshape(RANK, RANK)
    raw = slots[:, :, :SHARE].reshape(cols_local, RANK)
    factor_low = jnp.linalg.cholesky(gram_matrix)
    inverse_low = jax.scipy.linalg.solve_triangular(factor_low, jnp.eye(RANK, dtype=jnp.float32), lower=True)
    orthonormal = jnp.dot(power_left, inverse_low.T, precision=highest)
    power_right = jnp.dot(raw, inverse_low.T, precision=highest)
    sums = jnp.sum(power_right * power_right, axis=0, keepdims=True)
    sums = sums + lax.ppermute(sums, "c", [(0, 1), (1, 0)])
    column_sums = jnp.sum(gather_blocks(sums, "x", SIDE), axis=(0, 1))
    norm = lax.rsqrt(column_sums + 1e-06)
    share = jnp.dot(slot[:SHARE], inverse_low.T, precision=highest)
    momentum_out = blended - feedback_rate * jnp.dot(orthonormal, power_right.T, precision=highest)
    scale_factor = math.sqrt(D * FF / RANK)
    update = jnp.dot(orthonormal * (norm * scale_factor), power_right.T, precision=highest).astype(jnp.bfloat16)
    return (momentum_out, (share * norm).astype(jnp.bfloat16), update)


def solution(mesh):
    grid = Mesh(mesh.devices.reshape(SIDE, SIDE, SIDE, 2), ("z", "y", "x", "c"))
    mp, dp = ("z", "y"), ("x", "c")
    return jax.shard_map(
        local,
        mesh=grid,
        in_specs=(P(mp, dp), P(mp, dp), P((*dp, *mp), None)),
        out_specs=(P(mp, dp), P((*dp, *mp), None), P(mp, dp)),
        check_vma=False,
    )
```

time: 583 us -> 206 us (0.35)
  waiting for transfers between devices: 452 us -> 24.1 us
  starting transfers between devices: 0.12 us -> 44.2 us
  blocking collectives: 80.8 us -> 102 us
  between operations: 13.8 us -> 0.84 us
    psum x3 -> x0, waiting for transfers between devices: 452 us -> none  [the longest x1 170 us: local(): power_right = lax.psum(right_part, 'mp')]
    all_to_all x0 -> x6, blocking collectives: none -> 102 us  [exchange(): return lax.all_to_all(blocks, axis, 0, 0, tiled=False)]
    all_gather x1 -> x0, blocking collectives: 53 us -> none  [local(): lax.all_gather(factor_q, 'mp', axis=0, tiled=True).astype(jnp.float32)]
    psum x1 -> x0, blocking collectives: 27.8 us -> none  [local(): column_sums = lax.psum(jnp.sum(power_right * power_right, axis=0), 'dp')]
    all_to_all x0 -> x2, starting transfers between devices: none -> 27.4 us  [exchange(): return lax.all_to_all(blocks, axis, 0, 0, tiled=False)]
    all_to_all x0 -> x2, waiting for transfers between devices: none -> 22 us  [exchange(): return lax.all_to_all(blocks, axis, 0, 0, tiled=False)]
    ppermute x0 -> x3, starting transfers between devices: none -> 16.8 us  [the longest x1 6.89 us: local(): sums = sums + lax.ppermute(sums, 'c', [(0, 1), (1, 0)])]
  transfers between devices with their start and end apart: 3 -> 5, of which waited for: 3 -> 5; matrix products, arithmetic and copies ran while one was open for 0% -> 1% of each run, Pallas kernels for 0% -> 0%
where the time goes in v1:
time: 206 us
  blocking collectives  102 us (50%)
  starting transfers between devices  44.2 us (21%)
  waiting for transfers between devices  24.1 us (12%)
  other arithmetic  23.2 us (11%)
  matrix products  8.23 us (4%)
  local copies, waits for them, and re-layouts  2.74 us (1%)
    all_to_all x6, blocking collectives, exchange(): return lax.all_to_all(blocks, axis, 0, 0, tiled=False)  102 us
    all_to_all x2, starting transfers between devices, exchange(): return lax.all_to_all(blocks, axis, 0, 0, tiled=False)  27.4 us
    all_to_all x2, waiting for transfers between devices, exchange(): return lax.all_to_all(blocks, axis, 0, 0, tiled=False)  22 us
    another operation x3, other arithmetic, local(): factor_low = jnp.linalg.cholesky(gram_matrix)  12.4 us
    another operation x2, other arithmetic, local(): jax.scipy.linalg.solve_triangular(factor_low, jnp.eye(RANK, dtype=jnp.flo...  10.5 us
    ppermute x1, starting transfers between devices, local(): sums = sums + lax.ppermute(sums, 'c', [(0, 1), (1, 0)])  6.89 us
    ppermute x1, starting transfers between devices, sum_over_dp(): half = kept + lax.ppermute(given, 'c', [(0, 1), (1, 0)])  5.16 us
    ppermute x1, starting transfers between devices, sum_over_dp(): other = lax.ppermute(half, 'c', [(0, 1), (1, 0)])  4.77 us
  transfers between devices with their start and end apart: 5, of which 5 were waited for; matrix products, arithmetic and copies ran while one was open for 1% of the time, Pallas kernels for 0%

profile of v1, /device:TPU:1, one launch (start us, length us, event | category | flops | bytes accessed | tf_op | source)
XLA Modules:
  0.0 205.7 jit_solution(13575453042014955804)
XLA Ops:
  0.6 1.6 broadcast_in_dim.17
  2.2 24.1 %all-to-all-start = ((bf16[64,28,128]{2,1,0:T(8,128)(2,1)}), bf16[64,28,128]{2,1,0:T(8,128)(2,1)S(1)}, u32[]{:S(2)}, u32[]{:S(2)}) async-start(bf16[64,28,128]{2,1,0:T(8,128)(2,1)} %broadcast_in_dim.17), calls=%async_computation | async-start | bytes 1048576 | tf_op jit(solution)/shard_map/all_to_all | solution.py:21
  26.3 17.4 %all-to-all-done = bf16[64,28,128]{2,1,0:T(8,128)(2,1)S(1)} async-done(((bf16[64,28,128]{2,1,0:T(8,128)(2,1)}), bf16[64,28,128]{2,1,0:T(8,128)(2,1)S(1)}, u32[]{:S(2)}, u32[]{:S(2)}) %all-to-all-start) | async-done | bytes 458784 | tf_op jit(solution)/shard_map/all_to_all | solution.py:21
  43.8 0.6 fusion.3
  44.4 5.2 %collective-permute-start = (f32[64,128]{1,0:T(8,128)S(1)}, f32[64,128]{1,0:T(8,128)S(1)}, u32[]{:S(2)}, u32[]{:S(2)}) collective-permute-start(f32[64,128]{1,0:T(8,128)S(1)} %constant_dynamic-slice_fusion), channel_id=1, source_target_pairs={{0,1},{1,0},{2,3},{3,2},{4,5},{5,4},{6,7},{7,6},{8,9},{9,8},{10,11... | collective-permute-start | bytes 98312 | tf_op jit(solution)/shard_map/ppermute | solution.py:33
  49.6 0.8 collective-permute-done
  50.4 13.2 %all_to_all.40 = f32[8,8,128]{2,1,0:T(8,128)S(1)} all-to-all(f32[8,8,128]{2,1,0:T(8,128)S(1)} %add_bitcast_fusion), channel_id=1, replica_groups=mesh['z'=8,'y'=8,'x'=8,'c'=2] {'x'}, dimensions={0} | all-to-all | bytes 65536 | tf_op jit(solution)/shard_map/all_to_all | solution.py:21
  63.7 9.2 %all_to_all.41 = f32[8,8,128]{2,1,0:T(8,128)S(1)} all-to-all(f32[8,8,128]{2,1,0:T(8,128)S(1)} %broadcast_in_dim.19), channel_id=1, replica_groups=mesh['z'=8,'y'=8,'x'=8,'c'=2] {'x'}, dimensions={0} | all-to-all | bytes 65536 | tf_op jit(solution)/shard_map/all_to_all | solution.py:21
  72.9 4.8 %collective-permute-start.1 = (f32[64,128]{1,0:T(8,128)S(1)}, f32[64,128]{1,0:T(8,128)S(1)}, u32[]{:S(2)}, u32[]{:S(2)}) collective-permute-start(f32[64,128]{1,0:T(8,128)S(1)} %bitcast.34), channel_id=1, source_target_pairs={{0,1},{1,0},{2,3},{3,2},{4,5},{5,4},{6,7},{7,6},{8,9},{9,8},{10,11... | collective-permute-start | bytes 98312 | tf_op jit(solution)/shard_map/ppermute | solution.py:36
  77.8 0.7 collective-permute-done.1
  78.5 0.3 fusion.10
  78.8 1.6 fusion.2
  80.5 0.2 maximum_maximum_fusion
  80.7 31.1 %all_to_all.42 = f32[8,8,32,128]{3,2,1,0:T(8,128)S(1)} all-to-all(f32[8,8,32,128]{3,2,1,0:T(8,128)S(1)} %maximum_maximum_fusion), channel_id=1, replica_groups=mesh['z'=8,'y'=8,'x'=8,'c'=2] {'z'}, dimensions={0} | all-to-all | bytes 2097152 | tf_op jit(solution)/shard_map/all_to_all | solution.py:21
  111.8 11.4 %all_to_all.43 = f32[8,32,128]{2,1,0:T(8,128)S(1)} all-to-all(f32[8,32,128]{2,1,0:T(8,128)S(1)} %reduce_sum.46), channel_id=1, replica_groups=mesh['z'=8,'y'=8,'x'=8,'c'=2] {'y'}, dimensions={0} | all-to-all | bytes 262144 | tf_op jit(solution)/shard_map/all_to_all | solution.py:21
  123.3 10.4 %all_to_all.44 = f32[8,32,128]{2,1,0:T(8,128)S(1)} all-to-all(f32[8,32,128]{2,1,0:T(8,128)S(1)} %broadcast_in_dim.21), channel_id=1, replica_groups=mesh['z'=8,'y'=8,'x'=8,'c'=2] {'y'}, dimensions={0} | all-to-all | bytes 262144 | tf_op jit(solution)/shard_map/all_to_all | solution.py:21
  133.8 27.1 %all_to_all.45 = f32[8,8,32,128]{3,2,1,0:T(8,128)S(1)} all-to-all(f32[8,8,32,128]{3,2,1,0:T(8,128)S(1)} %broadcast_in_dim.22), channel_id=1, replica_groups=mesh['z'=8,'y'=8,'x'=8,'c'=2] {'z'}, dimensions={0} | all-to-all | bytes 2097152 | tf_op jit(solution)/shard_map/all_to_all | solution.py:21
  161.1 11.7 %cholesky.17 = f32[128,128]{1,0:T(8,128)S(1)} custom-call(f32[128,128]{1,0:T(8,128)S(1)} %fusion.7), custom_call_target="Cholesky" | custom-call | tf_op jit(solution)/shard_map/jit(cholesky)/cholesky | solution.py:62
  172.8 0.6 compare_reduce_fusion
  173.5 0.7 fusion.4
  174.2 9.8 %custom-call.7 = f32[1,128,128]{1,2,0:T(8,128)S(1)} custom-call(f32[1,128,128]{2,1,0:T(8,128)S(1)} %fusion.4), custom_call_target="InvertDiagBlocksLowerTriangular" | custom-call | tf_op jit(solution)/shard_map/jit(_solve_triangular)/triangular_solve | solution.py:63
  184.0 0.2 fusion.5
  184.3 0.9 multiply_reduce_fusion
  185.2 6.9 %collective-permute-start.2 = (f32[1,128]{1,0:T(1,128)S(1)}, f32[1,128]{1,0:T(1,128)S(1)}, u32[]{:S(2)}, u32[]{:S(2)}) collective-permute-start(f32[1,128]{1,0:T(1,128)S(1)} %bitcast.36), channel_id=1, source_target_pairs={{0,1},{1,0},{2,3},{3,2},{4,5},{5,4},{6,7},{7,6},{8,9},{9,8},{10,11... | collective-permute-start | bytes 1544 | tf_op jit(solution)/shard_map/ppermute | solution.py:67
  192.1 0.3 fusion.9
  192.4 0.5 collective-permute-done.2
  192.9 0.6 broadcast_in_dim.25
  193.5 3.3 %all-to-all-start.7 = ((f32[8,1,128]{2,1,0:T(1,128)}), f32[8,1,128]{2,1,0:T(1,128)S(1)}, u32[]{:S(2)}, u32[]{:S(2)}) async-start(f32[8,1,128]{2,1,0:T(1,128)} %broadcast_in_dim.25), calls=%async_computation.7 | async-start | bytes 8192 | tf_op jit(solution)/shard_map/all_to_all | solution.py:21
  196.8 1.8 fusion
  198.7 4.6 %all-to-all-done.7 = f32[8,1,128]{2,1,0:T(1,128)S(1)} async-done(((f32[8,1,128]{2,1,0:T(1,128)}), f32[8,1,128]{2,1,0:T(1,128)S(1)}, u32[]{:S(2)}, u32[]{:S(2)}) %all-to-all-start.7) | async-done | bytes 4128 | tf_op jit(solution)/shard_map/all_to_all | solution.py:21
  203.2 0.8 fusion.1
  204.1 1.7 convolution_convert_fusion
  (25 shorter events, 0.8 us)
Async XLA Ops:
  2.2 41.6 %copy-start = (f32[128,1792]{1,0:T(8,128)S(1)}, f32[128,1792]{1,0:T(8,128)}, u32[]{:S(2)}) copy-start(f32[128,1792]{1,0:T(8,128)} %param.3) | copy-start | bytes 2752516
  2.2 41.5 %all-to-all-start = ((bf16[64,28,128]{2,1,0:T(8,128)(2,1)}), bf16[64,28,128]{2,1,0:T(8,128)(2,1)S(1)}, u32[]{:S(2)}, u32[]{:S(2)}) async-start(bf16[64,28,128]{2,1,0:T(8,128)(2,1)} %broadcast_in_dim.17), calls=%async_computation | async-start | bytes 1048576 | tf_op jit(solution)/shard_map/all_to_all | solution.py:21
  26.3 17.5 %copy-start.1 = (bf16[128,1792]{1,0:T(8,128)(2,1)S(1)}, bf16[128,1792]{1,0:T(8,128)(2,1)}, u32[]{:S(2)}) copy-start(bf16[128,1792]{1,0:T(8,128)(2,1)} %param.4) | copy-start | bytes 1376260
  44.4 6.0 %collective-permute-start = (f32[64,128]{1,0:T(8,128)S(1)}, f32[64,128]{1,0:T(8,128)S(1)}, u32[]{:S(2)}, u32[]{:S(2)}) collective-permute-start(f32[64,128]{1,0:T(8,128)S(1)} %constant_dynamic-slice_fusion), channel_id=1, source_target_pairs={{0,1},{1,0},{2,3},{3,2},{4,5},{5,4},{6,7},{7,6},{8,9},{9,8},{10,11... | collective-permute-start | bytes 98312 | tf_op jit(solution)/shard_map/ppermute | solution.py:33
  72.9 5.6 %collective-permute-start.1 = (f32[64,128]{1,0:T(8,128)S(1)}, f32[64,128]{1,0:T(8,128)S(1)}, u32[]{:S(2)}, u32[]{:S(2)}) collective-permute-start(f32[64,128]{1,0:T(8,128)S(1)} %bitcast.34), channel_id=1, source_target_pairs={{0,1},{1,0},{2,3},{3,2},{4,5},{5,4},{6,7},{7,6},{8,9},{9,8},{10,11... | collective-permute-start | bytes 98312 | tf_op jit(solution)/shard_map/ppermute | solution.py:36
  185.2 7.7 %collective-permute-start.2 = (f32[1,128]{1,0:T(1,128)S(1)}, f32[1,128]{1,0:T(1,128)S(1)}, u32[]{:S(2)}, u32[]{:S(2)}) collective-permute-start(f32[1,128]{1,0:T(1,128)S(1)} %bitcast.36), channel_id=1, source_target_pairs={{0,1},{1,0},{2,3},{3,2},{4,5},{5,4},{6,7},{7,6},{8,9},{9,8},{10,11... | collective-permute-start | bytes 1544 | tf_op jit(solution)/shard_map/ppermute | solution.py:67
  193.5 9.7 %all-to-all-start.7 = ((f32[8,1,128]{2,1,0:T(1,128)}), f32[8,1,128]{2,1,0:T(1,128)S(1)}, u32[]{:S(2)}, u32[]{:S(2)}) async-start(f32[8,1,128]{2,1,0:T(1,128)} %broadcast_in_dim.25), calls=%async_computation.7 | async-start | bytes 8192 | tf_op jit(solution)/shard_map/all_to_all | solution.py:21

commit v2 on v1

v2 whole, which is shorter than its diff:
```python
import math

import jax
import jax.numpy as jnp
from jax import lax
from jax.experimental import pallas as pl
from jax.experimental.pallas import tpu as pltpu
from jax.sharding import Mesh
from jax.sharding import PartitionSpec as P

D = 8192
FF = 28672
RANK = 128
SIDE = 8
SHARE = 28
PANEL = 16

highest = lax.Precision.HIGHEST
feedback_rate = 0.05


def invert_low(gram_ref, out_ref, work_ref):
    rows = lax.broadcasted_iota(jnp.int32, (RANK, RANK), 0)
    lanes = lax.broadcasted_iota(jnp.int32, (RANK, RANK), 1)
    work_ref[:, :RANK] = gram_ref[...]
    work_ref[:, RANK:] = jnp.where(rows == lanes, 1.0, 0.0).astype(jnp.float32)
    own = lax.broadcasted_iota(jnp.int32, (PANEL, RANK), 0)
    for first in range(0, RANK, PANEL):
        last = first + PANEL
        panel = work_ref[first:last, :RANK]
        extra = work_ref[first:last, RANK:]
        cols = [jnp.broadcast_to(panel[:, first + t : first + t + 1], (PANEL, RANK)) for t in range(PANEL)]
        pivots = jnp.ones((PANEL, RANK), jnp.float32)
        for t in range(PANEL):
            pivot = jnp.broadcast_to(cols[t][t : t + 1], (PANEL, RANK))
            pivots = jnp.where(own == t, pivot, pivots)
            if t + 1 < PANEL:
                factor = jnp.where(own > t, cols[t] / pivot, 0.0)
                panel = panel - factor * panel[t : t + 1]
                extra = extra - factor * extra[t : t + 1]
                for u in range(t + 1, PANEL):
                    cols[u] = cols[u] - factor * cols[u][t : t + 1]
        out_ref[first:last] = extra * lax.rsqrt(pivots)
        if last < RANK:
            both = jnp.concatenate([panel, extra], axis=1)
            taken = lax.dot_general(
                panel / pivots,
                both,
                (((0,), (0,)), ((), ())),
                precision=highest,
                preferred_element_type=jnp.float32,
            )
            work_ref[last:] = work_ref[last:] - taken[last:]


def inverse_cholesky(gram_matrix):
    return pl.pallas_call(
        invert_low,
        out_shape=jax.ShapeDtypeStruct((RANK, RANK), jnp.float32),
        scratch_shapes=[pltpu.VMEM((RANK, 2 * RANK), jnp.float32)],
        name="invert_low",
    )(gram_matrix)


def exchange(blocks, axis):
    return lax.all_to_all(blocks, axis, 0, 0, tiled=False)


def gather_blocks(block, axis, size):
    return exchange(jnp.broadcast_to(block[None], (size, *block.shape)), axis)


def sum_over_dp(part):
    rows = part.shape[0] // 2
    core = lax.axis_index("c")
    kept = lax.dynamic_slice_in_dim(part, core * rows, rows, 0)
    given = lax.dynamic_slice_in_dim(part, (1 - core) * rows, rows, 0)
    half = kept + lax.ppermute(given, "c", [(0, 1), (1, 0)])
    half = jnp.sum(gather_blocks(half, "x", SIDE), axis=0)
    other = lax.ppermute(half, "c", [(0, 1), (1, 0)])
    low = jnp.where(core == 0, half, other)
    high = jnp.where(core == 0, other, half)
    return jnp.concatenate([low, high], axis=0)


def local(momentum, gradient, factor_q):
    blended = momentum + gradient.astype(jnp.float32)
    cols_local = blended.shape[1]
    q_cols = gather_blocks(factor_q, ("z", "y"), SIDE * SIDE).reshape(cols_local, RANK)
    power_left = sum_over_dp(jnp.dot(blended, q_cols.astype(jnp.float32), precision=highest))
    gram_part = jnp.dot(power_left.T, power_left, precision=highest)
    raw_part = jnp.dot(blended.T, power_left, precision=highest)
    slots = jnp.concatenate([raw_part.reshape(SIDE * SIDE, SHARE, RANK), gram_part.reshape(SIDE * SIDE, 2, RANK)], axis=1)
    slot = jnp.sum(exchange(slots, ("z", "y")), axis=0)
    slots = gather_blocks(slot, ("z", "y"), SIDE * SIDE)
    gram_matrix = slots[:, SHARE:].reshape(RANK, RANK)
    raw = slots[:, :SHARE].reshape(cols_local, RANK)
    inverse_low = inverse_cholesky(gram_matrix)
    orthonormal = jnp.dot(power_left, inverse_low.T, precision=highest)
    power_right = jnp.dot(raw, inverse_low.T, precision=highest)
    sums = jnp.sum(power_right * power_right, axis=0, keepdims=True)
    column_sums = jnp.sum(gather_blocks(sums, ("x", "c"), 2 * SIDE), axis=(0, 1))
    norm = lax.rsqrt(column_sums + 1e-06)
    share = jnp.dot(slot[:SHARE], inverse_low.T, precision=highest)
    momentum_out = blended - feedback_rate * jnp.dot(orthonormal, power_right.T, precision=highest)
    scale_factor = math.sqrt(D * FF / RANK)
    update = jnp.dot(orthonormal * (norm * scale_factor), power_right.T, precision=highest).astype(jnp.bfloat16)
    return (momentum_out, (share * norm).astype(jnp.bfloat16), update)


def solution(mesh):
    grid = Mesh(mesh.devices.reshape(SIDE, SIDE, SIDE, 2), ("z", "y", "x", "c"))
    mp, dp = ("z", "y"), ("x", "c")
    return jax.shard_map(
        local,
        mesh=grid,
        in_specs=(P(mp, dp), P(mp, dp), P((*dp, *mp), None)),
        out_specs=(P(mp, dp), P((*dp, *mp), None), P(mp, dp)),
        check_vma=False,
    )
```

time: 206 us -> 169 us (0.82)
  other arithmetic: 23.2 us -> 0.29 us
  blocking collectives: 102 us -> 83.5 us
  Pallas kernels: 0 us -> 6.3 us
  starting transfers between devices: 44.2 us -> 40.5 us
    another operation x5 -> x0, other arithmetic: 22.9 us -> none  [the longest x3 12.4 us: local(): factor_low = jnp.linalg.cholesky(gram_matrix)]
    all_to_all x6 -> x3, blocking collectives: 102 us -> 83.5 us  [exchange(): return lax.all_to_all(blocks, axis, 0, 0, tiled=False)]
    ppermute x1 -> x0, starting transfers between devices: 6.89 us -> none  [local(): sums = sums + lax.ppermute(sums, 'c', [(0, 1), (1, 0)])]
    pallas_call x0 -> x1, Pallas kernels: none -> 6.3 us  [inverse_cholesky(): pl.pallas_call(invert_low, out_shape=jax.ShapeDtypeStruct((RANK, RANK), j...]
    all_to_all x2, starting transfers between devices: 27.4 us -> 31.8 us  [exchange(): return lax.all_to_all(blocks, axis, 0, 0, tiled=False)]
  transfers between devices with their start and end apart: 5 -> 4, of which waited for: 5 -> 4; matrix products, arithmetic and copies ran while one was open for 1% -> 1% of each run, Pallas kernels for 0% -> 0%
where the time goes in v2:
time: 169 us; the launch traced here: 168 us
  blocking collectives  83.5 us (49%)
  starting transfers between devices  40.5 us (24%)
  waiting for transfers between devices  24.2 us (14%)
  matrix products  8.81 us (5%)
  Pallas kernels  6.3 us (4%)
  local copies, waits for them, and re-layouts  3.98 us (2%)
    all_to_all x3, blocking collectives, exchange(): return lax.all_to_all(blocks, axis, 0, 0, tiled=False)  83.5 us
    all_to_all x2, starting transfers between devices, exchange(): return lax.all_to_all(blocks, axis, 0, 0, tiled=False)  31.8 us
    all_to_all x2, waiting for transfers between devices, exchange(): return lax.all_to_all(blocks, axis, 0, 0, tiled=False)  22.6 us
    pallas_call x1, Pallas kernels, inverse_cholesky(): pl.pallas_call(invert_low, out_shape=jax.ShapeDtypeStruct((RANK, RANK), j...  6.3 us
    ppermute x1, starting transfers between devices, sum_over_dp(): half = kept + lax.ppermute(given, 'c', [(0, 1), (1, 0)])  5.16 us
    ppermute x1, starting transfers between devices, sum_over_dp(): other = lax.ppermute(half, 'c', [(0, 1), (1, 0)])  3.52 us
  transfers between devices with their start and end apart: 4, of which 4 were waited for; matrix products, arithmetic and copies ran while one was open for 1% of the time, Pallas kernels for 0%

profile of v2, /device:TPU:1, one launch (start us, length us, event | category | flops | bytes accessed | tf_op | source)
XLA Modules:
  0.0 168.4 jit_solution(14957881340756413518)
XLA Ops:
  0.6 1.6 broadcast_in_dim.8
  2.2 24.1 %all-to-all-start = ((bf16[64,28,128]{2,1,0:T(8,128)(2,1)}), bf16[64,28,128]{2,1,0:T(8,128)(2,1)S(1)}, u32[]{:S(2)}, u32[]{:S(2)}) async-start(bf16[64,28,128]{2,1,0:T(8,128)(2,1)} %broadcast_in_dim.8), calls=%async_computation | async-start | bytes 1048576 | tf_op jit(solution)/shard_map/all_to_all | solution.py:66
  26.3 0.0 copy-start.1
  26.3 17.4 %all-to-all-done = bf16[64,28,128]{2,1,0:T(8,128)(2,1)S(1)} async-done(((bf16[64,28,128]{2,1,0:T(8,128)(2,1)}), bf16[64,28,128]{2,1,0:T(8,128)(2,1)S(1)}, u32[]{:S(2)}, u32[]{:S(2)}) %all-to-all-start) | async-done | bytes 458784 | tf_op jit(solution)/shard_map/all_to_all | solution.py:66
  43.7 0.1 reshape.34
  43.8 0.0 copy-done
  43.8 0.6 fusion.3
  44.4 5.2 %collective-permute-start = (f32[64,128]{1,0:T(8,128)S(1)}, f32[64,128]{1,0:T(8,128)S(1)}, u32[]{:S(2)}, u32[]{:S(2)}) collective-permute-start(f32[64,128]{1,0:T(8,128)S(1)} %constant_dynamic-slice_fusion), channel_id=1, source_target_pairs={{0,1},{1,0},{2,3},{3,2},{4,5},{5,4},{6,7},{7,6},{8,9},{9,8},{10,11... | collective-permute-start | bytes 98312 | tf_op jit(solution)/shard_map/ppermute | solution.py:78
  49.6 0.8 collective-permute-done
  50.5 17.5 %all_to_all.25 = f32[8,64,128]{2,1,0:T(8,128)S(1)} all-to-all(f32[8,64,128]{2,1,0:T(8,128)S(1)} %broadcast_in_dim.9), channel_id=1, replica_groups=mesh['z'=8,'y'=8,'x'=8,'c'=2] {'x'}, dimensions={0} | all-to-all | bytes 524288 | tf_op jit(solution)/shard_map/all_to_all | solution.py:66
  68.0 3.5 %collective-permute-start.1 = (f32[64,128]{1,0:T(8,128)S(1)}, f32[64,128]{1,0:T(8,128)S(1)}, u32[]{:S(2)}, u32[]{:S(2)}) collective-permute-start(f32[64,128]{1,0:T(8,128)S(1)} %reduce_sum.36), channel_id=1, source_target_pairs={{0,1},{1,0},{2,3},{3,2},{4,5},{5,4},{6,7},{7,6},{8,9},{9,8},{10,11... | collective-permute-start | bytes 98312 | tf_op jit(solution)/shard_map/ppermute | solution.py:80
  71.5 0.8 collective-permute-done.1
  72.4 0.3 fusion.6
  72.7 1.6 fusion.2
  74.3 0.1 reshape.35
  74.3 0.1 pad_maximum_fusion
  74.5 32.3 %all_to_all.26 = f32[64,30,128]{2,1,0:T(8,128)S(1)} all-to-all(f32[64,30,128]{2,1,0:T(8,128)S(1)} %pad_maximum_fusion), channel_id=1, replica_groups=mesh['z'=8,'y'=8,'x'=8,'c'=2] {'z','y'}, dimensions={0} | all-to-all | bytes 1966080 | tf_op jit(solution)/shard_map/all_to_all | solution.py:66
  106.8 0.1 reduce_sum.37
  106.9 0.1 broadcast_in_dim.10
  107.1 33.6 %all_to_all.27 = f32[64,30,128]{2,1,0:T(8,128)S(1)} all-to-all(f32[64,30,128]{2,1,0:T(8,128)S(1)} %broadcast_in_dim.10), channel_id=1, replica_groups=mesh['z'=8,'y'=8,'x'=8,'c'=2] {'z','y'}, dimensions={0} | all-to-all | bytes 1966080 | tf_op jit(solution)/shard_map/all_to_all | solution.py:66
  140.7 0.7 slice.12
  141.4 6.3 %invert_low.1 = f32[128,128]{1,0:T(8,128)} custom-call(f32[128,128]{1,0:T(8,128)} %bitcast.14), custom_call_target="tpu_custom_call" | custom-call | tf_op jit(solution)/shard_map/invert_low/pallas_call | solution.py:57
  147.7 1.1 fusion.5
  148.8 0.1 reshape.38
  148.9 0.8 copy-done.2
  149.6 0.9 multiply_reduce_fusion
  150.5 0.6 broadcast_in_dim.11
  151.1 7.7 %all-to-all-start.4 = ((f32[16,1,128]{2,1,0:T(1,128)}), f32[16,1,128]{2,1,0:T(1,128)S(1)}, u32[]{:S(2)}, u32[]{:S(2)}) async-start(f32[16,1,128]{2,1,0:T(1,128)} %broadcast_in_dim.11), calls=%async_computation.4 | async-start | bytes 16384 | tf_op jit(solution)/shard_map/all_to_all | solution.py:66
  158.8 1.8 %fusion = f32[128,1792]{1,0:T(8,128)} fusion(f32[128,128]{1,0:T(8,128)S(1)} %fusion.5, f32[1792,128]{1,0:T(8,128)S(1)} %get-tuple-element.8, f32[128,1792]{1,0:T(8,128)S(1)} %copy-done, bf16[128,1792]{1,0:T(8,128)(2,1)S(1)} %copy-done.1), kind=kOutput, calls=%fused_computation.1 | convolution fusion | flops 353239040 | bytes 3276800 | tf_op jit(solution)/shard_map/dot_general | solution.py:105
  160.7 5.2 %all-to-all-done.4 = f32[16,1,128]{2,1,0:T(1,128)S(1)} async-done(((f32[16,1,128]{2,1,0:T(1,128)}), f32[16,1,128]{2,1,0:T(1,128)S(1)}, u32[]{:S(2)}, u32[]{:S(2)}) %all-to-all-start.4) | async-done | bytes 8224 | tf_op jit(solution)/shard_map/all_to_all | solution.py:66
  165.9 0.8 fusion.1
  166.7 1.7 convolution_convert_fusion
  (10 shorter events, 0.1 us)
Async XLA Ops:
  2.2 41.6 %copy-start = (f32[128,1792]{1,0:T(8,128)S(1)}, f32[128,1792]{1,0:T(8,128)}, u32[]{:S(2)}) copy-start(f32[128,1792]{1,0:T(8,128)} %param.3) | copy-start | bytes 2752516
  2.2 41.5 %all-to-all-start = ((bf16[64,28,128]{2,1,0:T(8,128)(2,1)}), bf16[64,28,128]{2,1,0:T(8,128)(2,1)S(1)}, u32[]{:S(2)}, u32[]{:S(2)}) async-start(bf16[64,28,128]{2,1,0:T(8,128)(2,1)} %broadcast_in_dim.8), calls=%async_computation | async-start | bytes 1048576 | tf_op jit(solution)/shard_map/all_to_all | solution.py:66
  26.3 17.5 %copy-start.1 = (bf16[128,1792]{1,0:T(8,128)(2,1)S(1)}, bf16[128,1792]{1,0:T(8,128)(2,1)}, u32[]{:S(2)}) copy-start(bf16[128,1792]{1,0:T(8,128)(2,1)} %param.4) | copy-start | bytes 1376260
  44.4 6.0 %collective-permute-start = (f32[64,128]{1,0:T(8,128)S(1)}, f32[64,128]{1,0:T(8,128)S(1)}, u32[]{:S(2)}, u32[]{:S(2)}) collective-permute-start(f32[64,128]{1,0:T(8,128)S(1)} %constant_dynamic-slice_fusion), channel_id=1, source_target_pairs={{0,1},{1,0},{2,3},{3,2},{4,5},{5,4},{6,7},{7,6},{8,9},{9,8},{10,11... | collective-permute-start | bytes 98312 | tf_op jit(solution)/shard_map/ppermute | solution.py:78
  68.0 4.4 %collective-permute-start.1 = (f32[64,128]{1,0:T(8,128)S(1)}, f32[64,128]{1,0:T(8,128)S(1)}, u32[]{:S(2)}, u32[]{:S(2)}) collective-permute-start(f32[64,128]{1,0:T(8,128)S(1)} %reduce_sum.36), channel_id=1, source_target_pairs={{0,1},{1,0},{2,3},{3,2},{4,5},{5,4},{6,7},{7,6},{8,9},{9,8},{10,11... | collective-permute-start | bytes 98312 | tf_op jit(solution)/shard_map/ppermute | solution.py:80
  148.8 0.8 copy-start.2
  151.1 14.7 %all-to-all-start.4 = ((f32[16,1,128]{2,1,0:T(1,128)}), f32[16,1,128]{2,1,0:T(1,128)S(1)}, u32[]{:S(2)}, u32[]{:S(2)}) async-start(f32[16,1,128]{2,1,0:T(1,128)} %broadcast_in_dim.11), calls=%async_computation.4 | async-start | bytes 16384 | tf_op jit(solution)/shard_map/all_to_all | solution.py:66

commit v3 on v2

--- a/solution.py
+++ b/solution.py
@@ -14,6 +14,15 @@
 SIDE = 8
 SHARE = 28
 PANEL = 16
+PART_SCALE = 2.0**-4
+SUM_SCALE = 2.0**-7
+GRAM_PART_SCALE = 2.0**-8
+GRAM_SUM_SCALE = 2.0**-11
+GRAM_FLOOR = 0.125
+SPREAD = 1.25
+HALF_NOISE = 4.4e-08
+NOISE_FLOOR = FF // 16 * 3.0e-16 * (1 + 64 * (SUM_SCALE / PART_SCALE) ** 2)
+NOISE_LIMIT = 1.6e-07
 
 highest = lax.Precision.HIGHEST
 feedback_rate = 0.05
@@ -83,29 +92,79 @@
     return jnp.concatenate([low, high], axis=0)
 
 
-def local(momentum, gradient, factor_q):
-    blended = momentum + gradient.astype(jnp.float32)
-    cols_local = blended.shape[1]
-    q_cols = gather_blocks(factor_q, ("z", "y"), SIDE * SIDE).reshape(cols_local, RANK)
-    power_left = sum_over_dp(jnp.dot(blended, q_cols.astype(jnp.float32), precision=highest))
-    gram_part = jnp.dot(power_left.T, power_left, precision=highest)
-    raw_part = jnp.dot(blended.T, power_left, precision=highest)
-    slots = jnp.concatenate([raw_part.reshape(SIDE * SIDE, SHARE, RANK), gram_part.reshape(SIDE * SIDE, 2, RANK)], axis=1)
-    slot = jnp.sum(exchange(slots, ("z", "y")), axis=0)
-    slots = gather_blocks(slot, ("z", "y"), SIDE * SIDE)
-    gram_matrix = slots[:, SHARE:].reshape(RANK, RANK)
-    raw = slots[:, :SHARE].reshape(cols_local, RANK)
-    inverse_low = inverse_cholesky(gram_matrix)
-    orthonormal = jnp.dot(power_left, inverse_low.T, precision=highest)
-    power_right = jnp.dot(raw, inverse_low.T, precision=highest)
-    sums = jnp.sum(power_right * power_right, axis=0, keepdims=True)
-    column_sums = jnp.sum(gather_blocks(sums, ("x", "c"), 2 * SIDE), axis=(0, 1))
-    norm = lax.rsqrt(column_sums + 1e-06)
-    share = jnp.dot(slot[:SHARE], inverse_low.T, precision=highest)
+def to_half(rows, gram_rows, row_scale, gram_scale):
+    gram_rows = gram_rows * gram_scale
+    high = lax.reduce_precision(gram_rows, 5, 10)
+    low = (gram_rows - high) * 2048.0
+    return jnp.concatenate([(v).astype(jnp.float16) for v in (rows * row_scale, high, low)], axis=1)
+
+
+def gram_of(packed, gram_scale):
+    high = packed[:, SHARE : SHARE + 2].astype(jnp.float32)
+    low = packed[:, SHARE + 2 :].astype(jnp.float32)
+    return (high + low * (1.0 / 2048.0)) * (1.0 / gram_scale)
+
+
+def outputs(blended, orthonormal, power_right, share, norm):
     momentum_out = blended - feedback_rate * jnp.dot(orthonormal, power_right.T, precision=highest)
     scale_factor = math.sqrt(D * FF / RANK)
     update = jnp.dot(orthonormal * (norm * scale_factor), power_right.T, precision=highest).astype(jnp.bfloat16)
     return (momentum_out, (share * norm).astype(jnp.bfloat16), update)
+
+
+def scales(column_sums):
+    return lax.rsqrt(column_sums + 1e-06)
+
+
+def full_precision(blended, power_left, raw_part, gram_part):
+    count = SIDE * SIDE
+    slots = jnp.concatenate([raw_part.reshape(count, SHARE, RANK), gram_part.reshape(count, 2, RANK)], axis=1)
+    slot = jnp.sum(exchange(slots, ("z", "y")), axis=0)
+    slots = gather_blocks(slot, ("z", "y"), count)
+    inverse_low = inverse_cholesky(slots[:, SHARE:].reshape(RANK, RANK))
+    orthonormal = jnp.dot(power_left, inverse_low.T, precision=highest)
+    power_right = jnp.dot(slots[:, :SHARE].reshape(count * SHARE, RANK), inverse_low.T, precision=highest)
+    sums = jnp.sum(power_right * power_right, axis=0, keepdims=True)
+    norm = scales(jnp.sum(gather_blocks(sums, ("x", "c"), 2 * SIDE), axis=(0, 1)))
+    share = jnp.dot(slot[:SHARE], inverse_low.T, precision=highest)
+    return outputs(blended, orthonormal, power_right, share, norm)
+
+
+def local(momentum, gradient, factor_q):
+    blended = momentum + gradient.astype(jnp.float32)
+    cols_local = blended.shape[1]
+    count = SIDE * SIDE
+    q_cols = gather_blocks(factor_q, ("z", "y"), count).reshape(cols_local, RANK)
+    power_left = sum_over_dp(jnp.dot(blended, q_cols.astype(jnp.float32), precision=highest))
+    gram_part = jnp.dot(power_left.T, power_left, precision=highest)
+    raw_part = jnp.dot(blended.T, power_left, precision=highest)
+    packed = to_half(raw_part.reshape(count, SHARE, RANK), gram_part.reshape(count, 2, RANK), PART_SCALE, GRAM_PART_SCALE)
+    packed = exchange(packed, ("z", "y"))
+    rows = packed[:, :SHARE].astype(jnp.float32)
+    total = jnp.sum(rows, axis=0)
+    cancelled = jnp.sum(rows * rows) > SPREAD * jnp.sum(total * total)
+    slot = jnp.where(cancelled, jnp.inf, total * (1.0 / PART_SCALE))
+    gram_slot = jnp.sum(gram_of(packed, GRAM_PART_SCALE), axis=0)
+    packed = gather_blocks(to_half(slot[None], gram_slot[None], SUM_SCALE, GRAM_SUM_SCALE)[0], ("z", "y"), count)
+    rows = lax.optimization_barrier(packed[:, :SHARE].reshape(cols_local, RANK)).astype(jnp.float32)
+    gram_rows = gram_of(packed, GRAM_SUM_SCALE)
+    gram_matrix = gram_rows.reshape(RANK, RANK)
+    inverse_low = inverse_cholesky(gram_matrix)
+    orthonormal = jnp.dot(power_left, inverse_low.T, precision=highest)
+    power_right = jnp.dot(rows, inverse_low.T * (1.0 / SUM_SCALE), precision=highest)
+    sums = jnp.sum(power_right * power_right, axis=0)
+    noise = jnp.sum(rows * rows, axis=0) * (HALF_NOISE * (1.0 + SPREAD)) + NOISE_FLOOR
+    noise = jnp.sum(inverse_low * inverse_low * noise, axis=1) * (1.0 / SUM_SCALE**2)
+    both = jnp.sum(gather_blocks(jnp.stack([sums, noise]), ("x", "c"), 2 * SIDE), axis=0)
+    norm = scales(both[0])
+    diagonal = jnp.max(jnp.where(jnp.eye(RANK, dtype=bool), gram_matrix, 0.0), axis=1)
+    fine = (jnp.mean(both[1] / both[0]) < NOISE_LIMIT) & (jnp.min(diagonal) > GRAM_FLOOR)
+    share = jnp.dot(slot, inverse_low.T, precision=highest)
+    return lax.cond(
+        fine,
+        lambda: outputs(blended, orthonormal, power_right, share, norm),
+        lambda: full_precision(blended, power_left, raw_part, gram_part),
+    )
 
 
 def solution(mesh):

time: 169 us -> 245 us (1.45)
  waiting for transfers between devices: 24.2 us -> 47.5 us
  blocking collectives: 83.5 us -> 105 us
  starting transfers between devices: 40.5 us -> 54.7 us
  Pallas kernels: 6.3 us -> 12.6 us
  other arithmetic: 0.29 us -> 4.8 us
  local copies, waits for them, and re-layouts: 3.98 us -> 7.47 us
  between operations: 0.78 us -> 3.5 us
    all_to_all x2 -> x4, waiting for transfers between devices: 22.6 us -> 45.9 us  [exchange(): return lax.all_to_all(blocks, axis, 0, 0, tiled=False)]
    all_to_all x3 -> x4, blocking collectives: 83.5 us -> 105 us  [exchange(): return lax.all_to_all(blocks, axis, 0, 0, tiled=False)]
    all_to_all x2 -> x4, starting transfers between devices: 31.8 us -> 46 us  [exchange(): return lax.all_to_all(blocks, axis, 0, 0, tiled=False)]
    pallas_call x1 -> x2, Pallas kernels: 6.3 us -> 12.6 us  [inverse_cholesky(): pl.pallas_call(invert_low, out_shape=jax.ShapeDtypeStruct((RANK, RANK), j...]
    reduce_sum x2 -> x9, other arithmetic: 0.12 us -> 2.68 us  [the longest x2 1.47 us: local(): cancelled = jnp.sum(rows * rows) > SPREAD * jnp.sum(total * total)]
    dot_general x4 -> x7, matrix products: 5.22 us -> 4.35 us  [the longest x1 1.01 us: outputs(): jnp.dot(orthonormal * (norm * scale_factor), power_right.T, precision=hig...]
  transfers between devices with their start and end apart: 4 -> 6, of which waited for: 4 -> 6; matrix products, arithmetic and copies ran while one was open for 1% -> 1% of each run, Pallas kernels for 0% -> 0%
where the time goes in v3:
time: 245 us; the launch traced here: 244 us
  blocking collectives  105 us (43%)
  starting transfers between devices  54.7 us (22%)
  waiting for transfers between devices  47.5 us (19%)
  Pallas kernels  12.6 us (5%)
  matrix products  7.89 us (3%)
  local copies, waits for them, and re-layouts  7.47 us (3%)
  other arithmetic  4.8 us (2%)
  between operations  3.5 us (1%)
    all_to_all x4, blocking collectives, exchange(): return lax.all_to_all(blocks, axis, 0, 0, tiled=False)  105 us
    all_to_all x4, starting transfers between devices, exchange(): return lax.all_to_all(blocks, axis, 0, 0, tiled=False)  46 us
    all_to_all x4, waiting for transfers between devices, exchange(): return lax.all_to_all(blocks, axis, 0, 0, tiled=False)  45.9 us
    pallas_call x2, Pallas kernels, inverse_cholesky(): pl.pallas_call(invert_low, out_shape=jax.ShapeDtypeStruct((RANK, RANK), j...  12.6 us
    ppermute x1, starting transfers between devices, sum_over_dp(): half = kept + lax.ppermute(given, 'c', [(0, 1), (1, 0)])  5.16 us
  transfers between devices with their start and end apart: 6, of which 6 were waited for; matrix products, arithmetic and copies ran while one was open for 1% of the time, Pallas kernels for 0%

profile of v3, /device:TPU:1, one launch (start us, length us, event | category | flops | bytes accessed | tf_op | source)
XLA Modules:
  0.0 244.1 jit_solution(6123205832880983773)
XLA Ops:
  0.6 1.6 broadcast_in_dim.22
  2.3 24.1 %all-to-all-start.3 = ((bf16[64,28,128]{2,1,0:T(8,128)(2,1)}), bf16[64,28,128]{2,1,0:T(8,128)(2,1)S(1)}, u32[]{:S(2)}, u32[]{:S(2)}) async-start(bf16[64,28,128]{2,1,0:T(8,128)(2,1)} %broadcast_in_dim.22), calls=%async_computation.3 | async-start | bytes 1048576 | tf_op jit(solution)/shard_map/all_to_all | solution.py:75
  26.5 17.3 %all-to-all-done.3 = bf16[64,28,128]{2,1,0:T(8,128)(2,1)S(1)} async-done(((bf16[64,28,128]{2,1,0:T(8,128)(2,1)}), bf16[64,28,128]{2,1,0:T(8,128)(2,1)S(1)}, u32[]{:S(2)}, u32[]{:S(2)}) %all-to-all-start.3) | async-done | bytes 458784 | tf_op jit(solution)/shard_map/all_to_all | solution.py:75
  44.5 5.2 %collective-permute-start = (f32[64,128]{1,0:T(8,128)S(1)}, f32[64,128]{1,0:T(8,128)S(1)}, u32[]{:S(2)}, u32[]{:S(2)}) collective-permute-start(f32[64,128]{1,0:T(8,128)S(1)} %constant_dynamic-slice_fusion), channel_id=1, source_target_pairs={{0,1},{1,0},{2,3},{3,2},{4,5},{5,4},{6,7},{7,6},{8,9},{9,8},{10,11... | collective-permute-start | bytes 98312 | tf_op jit(solution)/shard_map/ppermute | solution.py:87
  49.6 0.8 collective-permute-done
  50.5 17.5 %all_to_all.39 = f32[8,64,128]{2,1,0:T(8,128)S(1)} all-to-all(f32[8,64,128]{2,1,0:T(8,128)S(1)} %broadcast_in_dim.23), channel_id=1, replica_groups=mesh['z'=8,'y'=8,'x'=8,'c'=2] {'x'}, dimensions={0} | all-to-all | bytes 524288 | tf_op jit(solution)/shard_map/all_to_all | solution.py:75
  68.0 3.5 %collective-permute-start.1 = (f32[64,128]{1,0:T(8,128)S(1)}, f32[64,128]{1,0:T(8,128)S(1)}, u32[]{:S(2)}, u32[]{:S(2)}) collective-permute-start(f32[64,128]{1,0:T(8,128)S(1)} %reduce_sum.117), channel_id=1, source_target_pairs={{0,1},{1,0},{2,3},{3,2},{4,5},{5,4},{6,7},{7,6},{8,9},{9,8},{10,11... | collective-permute-start | bytes 98312 | tf_op jit(solution)/shard_map/ppermute | solution.py:89
  71.5 0.8 collective-permute-done.1
  72.7 1.6 multiply_convert_fusion
  74.9 22.1 %all_to_all.40 = f16[64,32,128]{2,1,0:T(8,128)(2,1)S(1)} all-to-all(f16[64,32,128]{2,1,0:T(8,128)(2,1)S(1)} %pad_maximum_fusion.1), channel_id=1, replica_groups=mesh['z'=8,'y'=8,'x'=8,'c'=2] {'z','y'}, dimensions={0} | all-to-all | bytes 1048576 | tf_op jit(solution)/shard_map/all_to_all | solution.py:75
  97.0 0.9 fusion.9
  99.9 0.9 broadcast_in_dim.26
  100.8 6.6 %all-to-all-start.6 = ((f16[64,32,128]{2,1,0:T(8,128)(2,1)}), f16[64,32,128]{2,1,0:T(8,128)(2,1)S(1)}, u32[]{:S(2)}, u32[]{:S(2)}) async-start(f16[64,32,128]{2,1,0:T(8,128)(2,1)} %broadcast_in_dim.26), calls=%async_computation.6 | async-start | bytes 1048576 | tf_op jit(solution)/shard_map/all_to_all | solution.py:75
  107.4 16.6 %all-to-all-done.6 = f16[64,32,128]{2,1,0:T(8,128)(2,1)S(1)} async-done(((f16[64,32,128]{2,1,0:T(8,128)(2,1)}), f16[64,32,128]{2,1,0:T(8,128)(2,1)S(1)}, u32[]{:S(2)}, u32[]{:S(2)}) %all-to-all-start.6) | async-done | bytes 524320 | tf_op jit(solution)/shard_map/all_to_all | solution.py:75
  124.0 0.7 fusion.12
  124.8 6.3 %invert_low.3 = f32[128,128]{1,0:T(8,128)} custom-call(f32[128,128]{1,0:T(8,128)} %bitcast.46), custom_call_target="tpu_custom_call" | custom-call | tf_op jit(solution)/shard_map/invert_low/pallas_call | solution.py:66
  131.0 1.1 fusion.27
  133.1 0.8 multiply_reduce_fusion.2
  134.7 7.2 %all-to-all-start.7 = ((f32[16,2,128]{2,1,0:T(2,128)}), f32[16,2,128]{2,1,0:T(2,128)S(1)}, u32[]{:S(2)}, u32[]{:S(2)}) async-start(f32[16,2,128]{2,1,0:T(2,128)} %broadcast_in_dim.27), calls=%async_computation.7 | async-start | bytes 32768 | tf_op jit(solution)/shard_map/all_to_all | solution.py:75
  143.4 5.9 %all-to-all-done.7 = f32[16,2,128]{2,1,0:T(2,128)S(1)} async-done(((f32[16,2,128]{2,1,0:T(2,128)}), f32[16,2,128]{2,1,0:T(2,128)S(1)}, u32[]{:S(2)}, u32[]{:S(2)}) %all-to-all-start.7) | async-done | bytes 16416 | tf_op jit(solution)/shard_map/all_to_all | solution.py:75
  150.6 92.5 %conditional.4 = (f32[128,1792]{1,0:T(8,128)S(1)}, bf16[128,1792]{1,0:T(8,128)(2,1)S(1)}, bf16[28,128]{1,0:T(8,128)(2,1)S(1)}) conditional(s32[]{:T(128)} %convert_element_type.101, (f32[1792,128]{1,0:T(8,128)S(1)}, f32[128,128]{1,0:T(8,128)S(1)}, f32[128,128]{1,0:T(8,128)S(1)}, f32[128,1792]{1,0:T(8,128)S(1)}) %tuple.25, ...), branch_computations={%region_12.16_spmd, %region_16.17_spmd} | conditional | flops 1089066240 | bytes 18448476
  151.0 32.3 %all_to_all.37 = f32[64,30,128]{2,1,0:T(8,128)S(1)} all-to-all(f32[64,30,128]{2,1,0:T(8,128)S(1)} %pad_maximum_fusion), channel_id=1, replica_groups=mesh['z'=8,'y'=8,'x'=8,'c'=2] {'z','y'}, dimensions={0} | all-to-all | bytes 1966080 | tf_op jit(solution)/shard_map/cond/branch_0_fun/all_to_all | solution.py:75
  183.5 33.4 %all_to_all.38 = f32[64,30,128]{2,1,0:T(8,128)S(1)} all-to-all(f32[64,30,128]{2,1,0:T(8,128)S(1)} %broadcast_in_dim.3), channel_id=1, replica_groups=mesh['z'=8,'y'=8,'x'=8,'c'=2] {'z','y'}, dimensions={0} | all-to-all | bytes 1966080 | tf_op jit(solution)/shard_map/cond/branch_0_fun/all_to_all | solution.py:75
  216.9 0.7 slice.42
  217.5 6.3 %invert_low.2 = f32[128,128]{1,0:T(8,128)} custom-call(f32[128,128]{1,0:T(8,128)} %bitcast.47), custom_call_target="tpu_custom_call" | custom-call | tf_op jit(solution)/shard_map/cond/branch_0_fun/invert_low/pallas_call | solution.py:66
  223.9 0.8 copy-done.1
  224.9 0.9 multiply_reduce_fusion
  226.5 8.1 %all-to-all-start.2 = ((f32[16,1,128]{2,1,0:T(1,128)}), f32[16,1,128]{2,1,0:T(1,128)S(1)}, u32[]{:S(2)}, u32[]{:S(2)}) async-start(f32[16,1,128]{2,1,0:T(1,128)} %broadcast_in_dim.4), calls=%async_computation.2 | async-start | bytes 16384 | tf_op jit(solution)/shard_map/cond/branch_0_fun/all_to_all | solution.py:75
  234.6 1.0 fusion
  235.5 6.0 %all-to-all-done.2 = f32[16,1,128]{2,1,0:T(1,128)S(1)} async-done(((f32[16,1,128]{2,1,0:T(1,128)}), f32[16,1,128]{2,1,0:T(1,128)S(1)}, u32[]{:S(2)}, u32[]{:S(2)}) %all-to-all-start.2) | async-done | bytes 8224 | tf_op jit(solution)/shard_map/cond/branch_0_fun/all_to_all | solution.py:75
  241.6 1.0 fusion.1
  243.1 0.9 copy-done.3
  (53 shorter events, 7.4 us)
Async XLA Ops:
  0.6 25.7 %copy-start.2 = (f32[128,1792]{1,0:T(8,128)S(1)}, f32[128,1792]{1,0:T(8,128)}, u32[]{:S(2)}) copy-start(f32[128,1792]{1,0:T(8,128)} %param.5) | copy-start | bytes 2752516
  2.3 24.1 %copy-start.4 = (bf16[128,1792]{1,0:T(8,128)(2,1)S(1)}, bf16[128,1792]{1,0:T(8,128)(2,1)}, u32[]{:S(2)}) copy-start(bf16[128,1792]{1,0:T(8,128)(2,1)} %param.6) | copy-start | bytes 1376260
  2.3 41.5 %all-to-all-start.3 = ((bf16[64,28,128]{2,1,0:T(8,128)(2,1)}), bf16[64,28,128]{2,1,0:T(8,128)(2,1)S(1)}, u32[]{:S(2)}, u32[]{:S(2)}) async-start(bf16[64,28,128]{2,1,0:T(8,128)(2,1)} %broadcast_in_dim.22), calls=%async_computation.3 | async-start | bytes 1048576 | tf_op jit(solution)/shard_map/all_to_all | solution.py:75
  44.5 6.0 %collective-permute-start = (f32[64,128]{1,0:T(8,128)S(1)}, f32[64,128]{1,0:T(8,128)S(1)}, u32[]{:S(2)}, u32[]{:S(2)}) collective-permute-start(f32[64,128]{1,0:T(8,128)S(1)} %constant_dynamic-slice_fusion), channel_id=1, source_target_pairs={{0,1},{1,0},{2,3},{3,2},{4,5},{5,4},{6,7},{7,6},{8,9},{9,8},{10,11... | collective-permute-start | bytes 98312 | tf_op jit(solution)/shard_map/ppermute | solution.py:87
  68.0 4.4 %collective-permute-start.1 = (f32[64,128]{1,0:T(8,128)S(1)}, f32[64,128]{1,0:T(8,128)S(1)}, u32[]{:S(2)}, u32[]{:S(2)}) collective-permute-start(f32[64,128]{1,0:T(8,128)S(1)} %reduce_sum.117), channel_id=1, source_target_pairs={{0,1},{1,0},{2,3},{3,2},{4,5},{5,4},{6,7},{7,6},{8,9},{9,8},{10,11... | collective-permute-start | bytes 98312 | tf_op jit(solution)/shard_map/ppermute | solution.py:89
  100.8 23.2 %all-to-all-start.6 = ((f16[64,32,128]{2,1,0:T(8,128)(2,1)}), f16[64,32,128]{2,1,0:T(8,128)(2,1)S(1)}, u32[]{:S(2)}, u32[]{:S(2)}) async-start(f16[64,32,128]{2,1,0:T(8,128)(2,1)} %broadcast_in_dim.26), calls=%async_computation.6 | async-start | bytes 1048576 | tf_op jit(solution)/shard_map/all_to_all | solution.py:75
  132.3 0.8 copy-start
  134.7 14.6 %all-to-all-start.7 = ((f32[16,2,128]{2,1,0:T(2,128)}), f32[16,2,128]{2,1,0:T(2,128)S(1)}, u32[]{:S(2)}, u32[]{:S(2)}) async-start(f32[16,2,128]{2,1,0:T(2,128)} %broadcast_in_dim.27), calls=%async_computation.7 | async-start | bytes 32768 | tf_op jit(solution)/shard_map/all_to_all | solution.py:75
  223.8 0.8 copy-start.1
  226.5 15.1 %all-to-all-start.2 = ((f32[16,1,128]{2,1,0:T(1,128)}), f32[16,1,128]{2,1,0:T(1,128)S(1)}, u32[]{:S(2)}, u32[]{:S(2)}) async-start(f32[16,1,128]{2,1,0:T(1,128)} %broadcast_in_dim.4), calls=%async_computation.2 | async-start | bytes 16384 | tf_op jit(solution)/shard_map/cond/branch_0_fun/all_to_all | solution.py:75
  243.1 0.9 copy-start.3
  243.1 1.1 copy-start.5
  243.1 1.1 copy-start.6

commit v4 on v3

--- a/solution.py
+++ b/solution.py
@@ -65,7 +65,7 @@
 def inverse_cholesky(gram_matrix):
     return pl.pallas_call(
         invert_low,
-        out_shape=jax.ShapeDtypeStruct((RANK, RANK), jnp.float32),
+        out_shape=pltpu.VMEM((RANK, RANK), jnp.float32),
         scratch_shapes=[pltpu.VMEM((RANK, 2 * RANK), jnp.float32)],
         name="invert_low",
     )(gram_matrix)
@@ -79,9 +79,8 @@
     return exchange(jnp.broadcast_to(block[None], (size, *block.shape)), axis)
 
 
-def sum_over_dp(part):
+def sum_over_dp(core, part):
     rows = part.shape[0] // 2
-    core = lax.axis_index("c")
     kept = lax.dynamic_slice_in_dim(part, core * rows, rows, 0)
     given = lax.dynamic_slice_in_dim(part, (1 - core) * rows, rows, 0)
     half = kept + lax.ppermute(given, "c", [(0, 1), (1, 0)])
@@ -131,19 +130,23 @@
 
 
 def local(momentum, gradient, factor_q):
+    cols_local = momentum.shape[1]
+    count = SIDE * SIDE
+    q_cols, core = lax.optimization_barrier((jnp.broadcast_to(factor_q[None], (count, SHARE, RANK)), lax.axis_index("c")))
+    q_cols = exchange(q_cols, ("z", "y"))
+    q_cols, momentum, gradient, core = lax.optimization_barrier((q_cols, momentum, gradient, core))
+    q_cols = q_cols.reshape(cols_local, RANK)
     blended = momentum + gradient.astype(jnp.float32)
-    cols_local = blended.shape[1]
-    count = SIDE * SIDE
-    q_cols = gather_blocks(factor_q, ("z", "y"), count).reshape(cols_local, RANK)
-    power_left = sum_over_dp(jnp.dot(blended, q_cols.astype(jnp.float32), precision=highest))
+    power_left = sum_over_dp(core, jnp.dot(blended, q_cols.astype(jnp.float32), precision=highest))
     gram_part = jnp.dot(power_left.T, power_left, precision=highest)
     raw_part = jnp.dot(blended.T, power_left, precision=highest)
     packed = to_half(raw_part.reshape(count, SHARE, RANK), gram_part.reshape(count, 2, RANK), PART_SCALE, GRAM_PART_SCALE)
     packed = exchange(packed, ("z", "y"))
     rows = packed[:, :SHARE].astype(jnp.float32)
     total = jnp.sum(rows, axis=0)
-    cancelled = jnp.sum(rows * rows) > SPREAD * jnp.sum(total * total)
-    slot = jnp.where(cancelled, jnp.inf, total * (1.0 / PART_SCALE))
+    energy = jnp.stack([jnp.sum(rows * rows, axis=(0, 1)), SPREAD * jnp.sum(total * total, axis=0)])
+    energy = jnp.dot(energy, jnp.ones((RANK, RANK), jnp.float32), precision=highest)
+    slot = jnp.where(energy[:1] > energy[1:], jnp.inf, total * (1.0 / PART_SCALE))
     gram_slot = jnp.sum(gram_of(packed, GRAM_PART_SCALE), axis=0)
     packed = gather_blocks(to_half(slot[None], gram_slot[None], SUM_SCALE, GRAM_SUM_SCALE)[0], ("z", "y"), count)
     rows = lax.optimization_barrier(packed[:, :SHARE].reshape(cols_local, RANK)).astype(jnp.float32)

time: 245 us -> 239 us (0.976)
  blocking collectives: 105 us -> 147 us
  starting transfers between devices: 54.7 us -> 30.6 us
  waiting for transfers between devices: 47.5 us -> 30.2 us
    all_to_all x4 -> x5, blocking collectives: 105 us -> 147 us  [exchange(): return lax.all_to_all(blocks, axis, 0, 0, tiled=False)]
    all_to_all x4 -> x3, starting transfers between devices: 46 us -> 21.9 us  [exchange(): return lax.all_to_all(blocks, axis, 0, 0, tiled=False)]
    all_to_all x4 -> x3, waiting for transfers between devices: 45.9 us -> 28.5 us  [exchange(): return lax.all_to_all(blocks, axis, 0, 0, tiled=False)]
  transfers between devices with their start and end apart: 6 -> 5, of which waited for: 6 -> 5; matrix products, arithmetic and copies ran while one was open for 1% -> 1% of each run, Pallas kernels for 0% -> 0%
where the time goes in v4:
time: 239 us; the launch traced here: 238 us
  blocking collectives  147 us (62%)
  starting transfers between devices  30.6 us (13%)
  waiting for transfers between devices  30.2 us (13%)
  Pallas kernels  11.3 us (5%)
  matrix products  7.19 us (3%)
  local copies, waits for them, and re-layouts  6.17 us (3%)
  other arithmetic  3.67 us (2%)
    all_to_all x5, blocking collectives, exchange(): return lax.all_to_all(blocks, axis, 0, 0, tiled=False)  147 us
    all_to_all x3, waiting for transfers between devices, exchange(): return lax.all_to_all(blocks, axis, 0, 0, tiled=False)  28.5 us
    all_to_all x3, starting transfers between devices, exchange(): return lax.all_to_all(blocks, axis, 0, 0, tiled=False)  21.9 us
    pallas_call x2, Pallas kernels, inverse_cholesky(): pl.pallas_call(invert_low, out_shape=pltpu.VMEM((RANK, RANK), jnp.float32...  11.3 us
    ppermute x1, starting transfers between devices, sum_over_dp(): half = kept + lax.ppermute(given, 'c', [(0, 1), (1, 0)])  5.16 us
  transfers between devices with their start and end apart: 5, of which 5 were waited for; matrix products, arithmetic and copies ran while one was open for 1% of the time, Pallas kernels for 0%

profile of v4, /device:TPU:1, one launch (start us, length us, event | category | flops | bytes accessed | tf_op | source)
XLA Modules:
  0.0 238.3 jit_solution(6289330795838817973)
XLA Ops:
  0.6 0.8 broadcast_in_dim.38
  1.4 41.3 %all_to_all.39 = bf16[64,28,128]{2,1,0:T(8,128)(2,1)S(1)} all-to-all(bf16[64,28,128]{2,1,0:T(8,128)(2,1)S(1)} %broadcast_in_dim.38), channel_id=1, replica_groups=mesh['z'=8,'y'=8,'x'=8,'c'=2] {'z','y'}, dimensions={0} | all-to-all | bytes 917504 | tf_op jit(solution)/shard_map/all_to_all | solution.py:75
  42.8 0.9 copy-done.2
  44.4 5.2 %collective-permute-start = (f32[64,128]{1,0:T(8,128)S(1)}, f32[64,128]{1,0:T(8,128)S(1)}, u32[]{:S(2)}, u32[]{:S(2)}) collective-permute-start(f32[64,128]{1,0:T(8,128)S(1)} %constant_dynamic-slice_fusion), channel_id=1, source_target_pairs={{0,1},{1,0},{2,3},{3,2},{4,5},{5,4},{6,7},{7,6},{8,9},{9,8},{10,11... | collective-permute-start | bytes 98312 | tf_op jit(solution)/shard_map/ppermute | solution.py:86
  49.6 0.8 collective-permute-done
  50.4 17.5 %all_to_all.40 = f32[8,64,128]{2,1,0:T(8,128)S(1)} all-to-all(f32[8,64,128]{2,1,0:T(8,128)S(1)} %broadcast_in_dim.49), channel_id=1, replica_groups=mesh['z'=8,'y'=8,'x'=8,'c'=2] {'x'}, dimensions={0} | all-to-all | bytes 524288 | tf_op jit(solution)/shard_map/all_to_all | solution.py:75
  67.9 3.5 %collective-permute-start.1 = (f32[64,128]{1,0:T(8,128)S(1)}, f32[64,128]{1,0:T(8,128)S(1)}, u32[]{:S(2)}, u32[]{:S(2)}) collective-permute-start(f32[64,128]{1,0:T(8,128)S(1)} %reduce_sum.117), channel_id=1, source_target_pairs={{0,1},{1,0},{2,3},{3,2},{4,5},{5,4},{6,7},{7,6},{8,9},{9,8},{10,11... | collective-permute-start | bytes 98312 | tf_op jit(solution)/shard_map/ppermute | solution.py:88
  71.5 0.8 collective-permute-done.1
  72.6 1.6 multiply_convert_fusion
  74.8 22.1 %all_to_all.41 = f16[64,32,128]{2,1,0:T(8,128)(2,1)S(1)} all-to-all(f16[64,32,128]{2,1,0:T(8,128)(2,1)S(1)} %pad_maximum_fusion.1), channel_id=1, replica_groups=mesh['z'=8,'y'=8,'x'=8,'c'=2] {'z','y'}, dimensions={0} | all-to-all | bytes 1048576 | tf_op jit(solution)/shard_map/all_to_all | solution.py:75
  97.6 0.9 broadcast_in_dim.76
  98.4 6.6 %all-to-all-start.6 = ((f16[64,32,128]{2,1,0:T(8,128)(2,1)}), f16[64,32,128]{2,1,0:T(8,128)(2,1)S(1)}, u32[]{:S(2)}, u32[]{:S(2)}) async-start(f16[64,32,128]{2,1,0:T(8,128)(2,1)} %broadcast_in_dim.76), calls=%async_computation.6 | async-start | bytes 1048576 | tf_op jit(solution)/shard_map/all_to_all | solution.py:75
  105.1 16.6 %all-to-all-done.6 = f16[64,32,128]{2,1,0:T(8,128)(2,1)S(1)} async-done(((f16[64,32,128]{2,1,0:T(8,128)(2,1)}), f16[64,32,128]{2,1,0:T(8,128)(2,1)S(1)}, u32[]{:S(2)}, u32[]{:S(2)}) %all-to-all-start.6) | async-done | bytes 524320 | tf_op jit(solution)/shard_map/all_to_all | solution.py:75
  121.7 0.7 fusion.12
  122.4 5.6 %invert_low.3 = f32[128,128]{1,0:T(8,128)S(1)} custom-call(f32[128,128]{1,0:T(8,128)} %bitcast.55), custom_call_target="tpu_custom_call" | custom-call | tf_op jit(solution)/shard_map/invert_low/pallas_call | solution.py:66
  128.7 0.8 multiply_reduce_fusion.2
  129.7 0.6 broadcast_in_dim.77
  130.3 7.2 %all-to-all-start.7 = ((f32[16,2,128]{2,1,0:T(2,128)}), f32[16,2,128]{2,1,0:T(2,128)S(1)}, u32[]{:S(2)}, u32[]{:S(2)}) async-start(f32[16,2,128]{2,1,0:T(2,128)} %broadcast_in_dim.77), calls=%async_computation.7 | async-start | bytes 32768 | tf_op jit(solution)/shard_map/all_to_all | solution.py:75
  137.7 0.6 reduce_min.9
  139.0 5.9 %all-to-all-done.7 = f32[16,2,128]{2,1,0:T(2,128)S(1)} async-done(((f32[16,2,128]{2,1,0:T(2,128)}), f32[16,2,128]{2,1,0:T(2,128)S(1)}, u32[]{:S(2)}, u32[]{:S(2)}) %all-to-all-start.7) | async-done | bytes 16416 | tf_op jit(solution)/shard_map/all_to_all | solution.py:75
  146.2 91.1 %conditional.4 = (f32[128,1792]{1,0:T(8,128)S(1)}, bf16[128,1792]{1,0:T(8,128)(2,1)S(1)}, bf16[28,128]{1,0:T(8,128)(2,1)S(1)}) conditional(s32[]{:T(128)} %convert_element_type.97, (f32[1792,128]{1,0:T(8,128)S(1)}, f32[128,128]{1,0:T(8,128)S(1)}, f32[128,128]{1,0:T(8,128)S(1)}, f32[128,1792]{1,0:T(8,128)S(1)}) %tuple.29, ...), branch_computations={%region_12.16_spmd, %region_16.17_spmd} | conditional | flops 1089066240 | bytes 18186304
  146.6 32.3 %all_to_all.37 = f32[64,30,128]{2,1,0:T(8,128)S(1)} all-to-all(f32[64,30,128]{2,1,0:T(8,128)S(1)} %pad_maximum_fusion), channel_id=1, replica_groups=mesh['z'=8,'y'=8,'x'=8,'c'=2] {'z','y'}, dimensions={0} | all-to-all | bytes 1966080 | tf_op jit(solution)/shard_map/cond/branch_0_fun/all_to_all | solution.py:75
  179.1 33.4 %all_to_all.38 = f32[64,30,128]{2,1,0:T(8,128)S(1)} all-to-all(f32[64,30,128]{2,1,0:T(8,128)S(1)} %broadcast_in_dim.8), channel_id=1, replica_groups=mesh['z'=8,'y'=8,'x'=8,'c'=2] {'z','y'}, dimensions={0} | all-to-all | bytes 1966080 | tf_op jit(solution)/shard_map/cond/branch_0_fun/all_to_all | solution.py:75
  212.5 0.7 slice.50
  213.1 5.6 %invert_low.2 = f32[128,128]{1,0:T(8,128)S(1)} custom-call(f32[128,128]{1,0:T(8,128)} %bitcast.56), custom_call_target="tpu_custom_call" | custom-call | tf_op jit(solution)/shard_map/cond/branch_0_fun/invert_low/pallas_call | solution.py:66
  219.1 0.9 multiply_reduce_fusion
  220.0 0.6 broadcast_in_dim.9
  220.6 8.1 %all-to-all-start.2 = ((f32[16,1,128]{2,1,0:T(1,128)}), f32[16,1,128]{2,1,0:T(1,128)S(1)}, u32[]{:S(2)}, u32[]{:S(2)}) async-start(f32[16,1,128]{2,1,0:T(1,128)} %broadcast_in_dim.9), calls=%async_computation.2 | async-start | bytes 16384 | tf_op jit(solution)/shard_map/cond/branch_0_fun/all_to_all | solution.py:75
  228.8 1.0 fusion
  229.7 6.0 %all-to-all-done.2 = f32[16,1,128]{2,1,0:T(1,128)S(1)} async-done(((f32[16,1,128]{2,1,0:T(1,128)}), f32[16,1,128]{2,1,0:T(1,128)S(1)}, u32[]{:S(2)}, u32[]{:S(2)}) %all-to-all-start.2) | async-done | bytes 8224 | tf_op jit(solution)/shard_map/cond/branch_0_fun/all_to_all | solution.py:75
  235.8 1.0 fusion.1
  237.3 0.9 copy-done.1
  (51 shorter events, 5.1 us)
Async XLA Ops:
  1.4 41.4 %copy-start = (f32[128,1792]{1,0:T(8,128)S(1)}, f32[128,1792]{1,0:T(8,128)}, u32[]{:S(2)}) copy-start(f32[128,1792]{1,0:T(8,128)} %param.5) | copy-start | bytes 2752516
  42.7 1.0 copy-start.2
  44.4 6.0 %collective-permute-start = (f32[64,128]{1,0:T(8,128)S(1)}, f32[64,128]{1,0:T(8,128)S(1)}, u32[]{:S(2)}, u32[]{:S(2)}) collective-permute-start(f32[64,128]{1,0:T(8,128)S(1)} %constant_dynamic-slice_fusion), channel_id=1, source_target_pairs={{0,1},{1,0},{2,3},{3,2},{4,5},{5,4},{6,7},{7,6},{8,9},{9,8},{10,11... | collective-permute-start | bytes 98312 | tf_op jit(solution)/shard_map/ppermute | solution.py:86
  67.9 4.4 %collective-permute-start.1 = (f32[64,128]{1,0:T(8,128)S(1)}, f32[64,128]{1,0:T(8,128)S(1)}, u32[]{:S(2)}, u32[]{:S(2)}) collective-permute-start(f32[64,128]{1,0:T(8,128)S(1)} %reduce_sum.117), channel_id=1, source_target_pairs={{0,1},{1,0},{2,3},{3,2},{4,5},{5,4},{6,7},{7,6},{8,9},{9,8},{10,11... | collective-permute-start | bytes 98312 | tf_op jit(solution)/shard_map/ppermute | solution.py:88
  98.4 23.2 %all-to-all-start.6 = ((f16[64,32,128]{2,1,0:T(8,128)(2,1)}), f16[64,32,128]{2,1,0:T(8,128)(2,1)S(1)}, u32[]{:S(2)}, u32[]{:S(2)}) async-start(f16[64,32,128]{2,1,0:T(8,128)(2,1)} %broadcast_in_dim.76), calls=%async_computation.6 | async-start | bytes 1048576 | tf_op jit(solution)/shard_map/all_to_all | solution.py:75
  130.3 14.6 %all-to-all-start.7 = ((f32[16,2,128]{2,1,0:T(2,128)}), f32[16,2,128]{2,1,0:T(2,128)S(1)}, u32[]{:S(2)}, u32[]{:S(2)}) async-start(f32[16,2,128]{2,1,0:T(2,128)} %broadcast_in_dim.77), calls=%async_computation.7 | async-start | bytes 32768 | tf_op jit(solution)/shard_map/all_to_all | solution.py:75
  220.6 15.1 %all-to-all-start.2 = ((f32[16,1,128]{2,1,0:T(1,128)}), f32[16,1,128]{2,1,0:T(1,128)S(1)}, u32[]{:S(2)}, u32[]{:S(2)}) async-start(f32[16,1,128]{2,1,0:T(1,128)} %broadcast_in_dim.9), calls=%async_computation.2 | async-start | bytes 16384 | tf_op jit(solution)/shard_map/cond/branch_0_fun/all_to_all | solution.py:75
  237.3 0.9 copy-start.1
  237.3 1.1 copy-start.3
  237.3 1.1 copy-start.4

commit v5 on v4

--- a/solution.py
+++ b/solution.py
@@ -25,6 +25,7 @@
 NOISE_LIMIT = 1.6e-07
 
 highest = lax.Precision.HIGHEST
+high = lax.Precision.HIGH
 feedback_rate = 0.05
 
 
@@ -93,9 +94,9 @@
 
 def to_half(rows, gram_rows, row_scale, gram_scale):
     gram_rows = gram_rows * gram_scale
-    high = lax.reduce_precision(gram_rows, 5, 10)
-    low = (gram_rows - high) * 2048.0
-    return jnp.concatenate([(v).astype(jnp.float16) for v in (rows * row_scale, high, low)], axis=1)
+    coarse = lax.reduce_precision(gram_rows, 5, 10)
+    fine = (gram_rows - coarse) * 2048.0
+    return jnp.concatenate([v.astype(jnp.float16) for v in (rows * row_scale, coarse, fine)], axis=1)
 
 
 def gram_of(packed, gram_scale):
@@ -105,9 +106,9 @@
 
 
 def outputs(blended, orthonormal, power_right, share, norm):
-    momentum_out = blended - feedback_rate * jnp.dot(orthonormal, power_right.T, precision=highest)
+    momentum_out = blended - feedback_rate * jnp.dot(orthonormal, power_right.T, precision=high)
     scale_factor = math.sqrt(D * FF / RANK)
-    update = jnp.dot(orthonormal * (norm * scale_factor), power_right.T, precision=highest).astype(jnp.bfloat16)
+    update = jnp.dot(orthonormal * (norm * scale_factor), power_right.T, precision=high).astype(jnp.bfloat16)
     return (momentum_out, (share * norm).astype(jnp.bfloat16), update)
 
 
@@ -115,8 +116,9 @@
     return lax.rsqrt(column_sums + 1e-06)
 
 
-def full_precision(blended, power_left, raw_part, gram_part):
+def full_precision(blended, power_left, gram_part):
     count = SIDE * SIDE
+    raw_part = jnp.dot(blended.T, power_left, precision=highest)
     slots = jnp.concatenate([raw_part.reshape(count, SHARE, RANK), gram_part.reshape(count, 2, RANK)], axis=1)
     slot = jnp.sum(exchange(slots, ("z", "y")), axis=0)
     slots = gather_blocks(slot, ("z", "y"), count)
@@ -134,12 +136,12 @@
     count = SIDE * SIDE
     q_cols, core = lax.optimization_barrier((jnp.broadcast_to(factor_q[None], (count, SHARE, RANK)), lax.axis_index("c")))
     q_cols = exchange(q_cols, ("z", "y"))
-    q_cols, momentum, gradient, core = lax.optimization_barrier((q_cols, momentum, gradient, core))
+    q_cols, momentum, core = lax.optimization_barrier((q_cols, momentum, core))
     q_cols = q_cols.reshape(cols_local, RANK)
     blended = momentum + gradient.astype(jnp.float32)
     power_left = sum_over_dp(core, jnp.dot(blended, q_cols.astype(jnp.float32), precision=highest))
     gram_part = jnp.dot(power_left.T, power_left, precision=highest)
-    raw_part = jnp.dot(blended.T, power_left, precision=highest)
+    raw_part = jnp.dot(blended.T, power_left, precision=high)
     packed = to_half(raw_part.reshape(count, SHARE, RANK), gram_part.reshape(count, 2, RANK), PART_SCALE, GRAM_PART_SCALE)
     packed = exchange(packed, ("z", "y"))
     rows = packed[:, :SHARE].astype(jnp.float32)
@@ -154,7 +156,7 @@
     gram_matrix = gram_rows.reshape(RANK, RANK)
     inverse_low = inverse_cholesky(gram_matrix)
     orthonormal = jnp.dot(power_left, inverse_low.T, precision=highest)
-    power_right = jnp.dot(rows, inverse_low.T * (1.0 / SUM_SCALE), precision=highest)
+    power_right = jnp.dot(rows, inverse_low.T * (1.0 / SUM_SCALE), precision=high)
     sums = jnp.sum(power_right * power_right, axis=0)
     noise = jnp.sum(rows * rows, axis=0) * (HALF_NOISE * (1.0 + SPREAD)) + NOISE_FLOOR
     noise = jnp.sum(inverse_low * inverse_low * noise, axis=1) * (1.0 / SUM_SCALE**2)
@@ -166,7 +168,7 @@
     return lax.cond(
         fine,
         lambda: outputs(blended, orthonormal, power_right, share, norm),
-        lambda: full_precision(blended, power_left, raw_part, gram_part),
+        lambda: full_precision(blended, power_left, gram_part),
     )
 
 

time: 239 us -> 240 us (level)
  no operation moved by 1% of the time
where the time goes in v5:
time: 240 us; the launch traced here: 239 us
  blocking collectives  147 us (61%)
  starting transfers between devices  30.6 us (13%)
  waiting for transfers between devices  30.6 us (13%)
  Pallas kernels  11.3 us (5%)
  matrix products  7.13 us (3%)
  local copies, waits for them, and re-layouts  6.75 us (3%)
  other arithmetic  3.67 us (2%)
    all_to_all x5, blocking collectives, exchange(): return lax.all_to_all(blocks, axis, 0, 0, tiled=False)  147 us
    all_to_all x3, waiting for transfers between devices, exchange(): return lax.all_to_all(blocks, axis, 0, 0, tiled=False)  28.9 us
    all_to_all x3, starting transfers between devices, exchange(): return lax.all_to_all(blocks, axis, 0, 0, tiled=False)  21.9 us
    pallas_call x2, Pallas kernels, inverse_cholesky(): pl.pallas_call(invert_low, out_shape=pltpu.VMEM((RANK, RANK), jnp.float32...  11.3 us
    ppermute x1, starting transfers between devices, sum_over_dp(): half = kept + lax.ppermute(given, 'c', [(0, 1), (1, 0)])  5.16 us
  transfers between devices with their start and end apart: 5, of which 5 were waited for; matrix products, arithmetic and copies ran while one was open for 1% of the time, Pallas kernels for 0%

profile of v5, /device:TPU:1, one launch (start us, length us, event | category | flops | bytes accessed | tf_op | source)
XLA Modules:
  0.0 239.2 jit_solution(10313048168939695335)
XLA Ops:
  0.6 0.8 broadcast_in_dim.38
  1.4 41.3 %all_to_all.39 = bf16[64,28,128]{2,1,0:T(8,128)(2,1)S(1)} all-to-all(bf16[64,28,128]{2,1,0:T(8,128)(2,1)S(1)} %broadcast_in_dim.38), channel_id=1, replica_groups=mesh['z'=8,'y'=8,'x'=8,'c'=2] {'z','y'}, dimensions={0} | all-to-all | bytes 917504 | tf_op jit(solution)/shard_map/all_to_all | solution.py:76
  42.8 0.9 copy-done.2
  44.4 5.2 %collective-permute-start = (f32[64,128]{1,0:T(8,128)S(1)}, f32[64,128]{1,0:T(8,128)S(1)}, u32[]{:S(2)}, u32[]{:S(2)}) collective-permute-start(f32[64,128]{1,0:T(8,128)S(1)} %constant_dynamic-slice_fusion), channel_id=1, source_target_pairs={{0,1},{1,0},{2,3},{3,2},{4,5},{5,4},{6,7},{7,6},{8,9},{9,8},{10,11... | collective-permute-start | bytes 98312 | tf_op jit(solution)/shard_map/ppermute | solution.py:87
  49.6 0.8 collective-permute-done
  50.4 17.5 %all_to_all.40 = f32[8,64,128]{2,1,0:T(8,128)S(1)} all-to-all(f32[8,64,128]{2,1,0:T(8,128)S(1)} %broadcast_in_dim.49), channel_id=1, replica_groups=mesh['z'=8,'y'=8,'x'=8,'c'=2] {'x'}, dimensions={0} | all-to-all | bytes 524288 | tf_op jit(solution)/shard_map/all_to_all | solution.py:76
  67.9 3.5 %collective-permute-start.1 = (f32[64,128]{1,0:T(8,128)S(1)}, f32[64,128]{1,0:T(8,128)S(1)}, u32[]{:S(2)}, u32[]{:S(2)}) collective-permute-start(f32[64,128]{1,0:T(8,128)S(1)} %reduce_sum.117), channel_id=1, source_target_pairs={{0,1},{1,0},{2,3},{3,2},{4,5},{5,4},{6,7},{7,6},{8,9},{9,8},{10,11... | collective-permute-start | bytes 98312 | tf_op jit(solution)/shard_map/ppermute | solution.py:89
  71.5 0.8 collective-permute-done.1
  72.6 0.9 fusion.9
  74.1 22.1 %all_to_all.41 = f16[64,32,128]{2,1,0:T(8,128)(2,1)S(1)} all-to-all(f16[64,32,128]{2,1,0:T(8,128)(2,1)S(1)} %pad_maximum_fusion.1), channel_id=1, replica_groups=mesh['z'=8,'y'=8,'x'=8,'c'=2] {'z','y'}, dimensions={0} | all-to-all | bytes 1048576 | tf_op jit(solution)/shard_map/all_to_all | solution.py:76
  96.9 0.9 broadcast_in_dim.76
  97.7 6.6 %all-to-all-start.6 = ((f16[64,32,128]{2,1,0:T(8,128)(2,1)}), f16[64,32,128]{2,1,0:T(8,128)(2,1)S(1)}, u32[]{:S(2)}, u32[]{:S(2)}) async-start(f16[64,32,128]{2,1,0:T(8,128)(2,1)} %broadcast_in_dim.76), calls=%async_computation.6 | async-start | bytes 1048576 | tf_op jit(solution)/shard_map/all_to_all | solution.py:76
  104.3 16.6 %all-to-all-done.6 = f16[64,32,128]{2,1,0:T(8,128)(2,1)S(1)} async-done(((f16[64,32,128]{2,1,0:T(8,128)(2,1)}), f16[64,32,128]{2,1,0:T(8,128)(2,1)S(1)}, u32[]{:S(2)}, u32[]{:S(2)}) %all-to-all-start.6) | async-done | bytes 524320 | tf_op jit(solution)/shard_map/all_to_all | solution.py:76
  121.0 0.7 fusion.13
  121.7 5.6 %invert_low.3 = f32[128,128]{1,0:T(8,128)S(1)} custom-call(f32[128,128]{1,0:T(8,128)} %bitcast.57), custom_call_target="tpu_custom_call" | custom-call | tf_op jit(solution)/shard_map/invert_low/pallas_call | solution.py:67
  128.7 0.6 broadcast_in_dim.77
  129.3 7.2 %all-to-all-start.7 = ((f32[16,2,128]{2,1,0:T(2,128)}), f32[16,2,128]{2,1,0:T(2,128)S(1)}, u32[]{:S(2)}, u32[]{:S(2)}) async-start(f32[16,2,128]{2,1,0:T(2,128)} %broadcast_in_dim.77), calls=%async_computation.7 | async-start | bytes 32768 | tf_op jit(solution)/shard_map/all_to_all | solution.py:76
  136.7 0.6 reduce_min.9
  138.0 5.9 %all-to-all-done.7 = f32[16,2,128]{2,1,0:T(2,128)S(1)} async-done(((f32[16,2,128]{2,1,0:T(2,128)}), f32[16,2,128]{2,1,0:T(2,128)S(1)}, u32[]{:S(2)}, u32[]{:S(2)}) %all-to-all-start.7) | async-done | bytes 16416 | tf_op jit(solution)/shard_map/all_to_all | solution.py:76
  143.9 0.6 fusion.30
  145.8 92.4 %conditional.4 = (f32[128,1792]{1,0:T(8,128)S(1)}, bf16[128,1792]{1,0:T(8,128)(2,1)S(1)}, bf16[28,128]{1,0:T(8,128)(2,1)S(1)}) conditional(s32[]{:T(128)} %convert_element_type.97, (f32[128,1792]{1,0:T(8,128)S(1)}, f32[128,128]{1,0:T(8,128)S(1)}, f32[128,128]{1,0:T(8,128)S(1)}) %tuple.29, (f32[128,128]{1,0:T(8,128)S(1)}, ...), branch_computations={%region_12.16_spmd, %region_16.17_spmd} | conditional | flops 1089066240 | bytes 20086848
  146.0 1.6 fusion.38
  147.8 32.3 %all_to_all.37 = f32[64,30,128]{2,1,0:T(8,128)S(1)} all-to-all(f32[64,30,128]{2,1,0:T(8,128)S(1)} %pad_maximum_fusion), channel_id=1, replica_groups=mesh['z'=8,'y'=8,'x'=8,'c'=2] {'z','y'}, dimensions={0} | all-to-all | bytes 1966080 | tf_op jit(solution)/shard_map/cond/branch_0_fun/all_to_all | solution.py:76
  180.3 33.4 %all_to_all.38 = f32[64,30,128]{2,1,0:T(8,128)S(1)} all-to-all(f32[64,30,128]{2,1,0:T(8,128)S(1)} %broadcast_in_dim.8), channel_id=1, replica_groups=mesh['z'=8,'y'=8,'x'=8,'c'=2] {'z','y'}, dimensions={0} | all-to-all | bytes 1966080 | tf_op jit(solution)/shard_map/cond/branch_0_fun/all_to_all | solution.py:76
  213.7 0.7 slice.50
  214.4 5.6 %invert_low.2 = f32[128,128]{1,0:T(8,128)S(1)} custom-call(f32[128,128]{1,0:T(8,128)} %bitcast.58), custom_call_target="tpu_custom_call" | custom-call | tf_op jit(solution)/shard_map/cond/branch_0_fun/invert_low/pallas_call | solution.py:67
  220.4 0.9 multiply_reduce_fusion
  221.3 0.6 broadcast_in_dim.9
  221.9 8.1 %all-to-all-start.2 = ((f32[16,1,128]{2,1,0:T(1,128)}), f32[16,1,128]{2,1,0:T(1,128)S(1)}, u32[]{:S(2)}, u32[]{:S(2)}) async-start(f32[16,1,128]{2,1,0:T(1,128)} %broadcast_in_dim.9), calls=%async_computation.2 | async-start | bytes 16384 | tf_op jit(solution)/shard_map/cond/branch_0_fun/all_to_all | solution.py:76
  230.6 6.4 %all-to-all-done.2 = f32[16,1,128]{2,1,0:T(1,128)S(1)} async-done(((f32[16,1,128]{2,1,0:T(1,128)}), f32[16,1,128]{2,1,0:T(1,128)S(1)}, u32[]{:S(2)}, u32[]{:S(2)}) %all-to-all-start.2) | async-done | bytes 8224 | tf_op jit(solution)/shard_map/cond/branch_0_fun/all_to_all | solution.py:76
  237.0 0.7 fusion.1
  238.2 0.9 copy-done.1
  (52 shorter events, 6.2 us)
Async XLA Ops:
  1.4 41.4 %copy-start = (f32[128,1792]{1,0:T(8,128)S(1)}, f32[128,1792]{1,0:T(8,128)}, u32[]{:S(2)}) copy-start(f32[128,1792]{1,0:T(8,128)} %param.5) | copy-start | bytes 2752516
  42.7 1.0 copy-start.2
  44.4 6.0 %collective-permute-start = (f32[64,128]{1,0:T(8,128)S(1)}, f32[64,128]{1,0:T(8,128)S(1)}, u32[]{:S(2)}, u32[]{:S(2)}) collective-permute-start(f32[64,128]{1,0:T(8,128)S(1)} %constant_dynamic-slice_fusion), channel_id=1, source_target_pairs={{0,1},{1,0},{2,3},{3,2},{4,5},{5,4},{6,7},{7,6},{8,9},{9,8},{10,11... | collective-permute-start | bytes 98312 | tf_op jit(solution)/shard_map/ppermute | solution.py:87
  67.9 4.4 %collective-permute-start.1 = (f32[64,128]{1,0:T(8,128)S(1)}, f32[64,128]{1,0:T(8,128)S(1)}, u32[]{:S(2)}, u32[]{:S(2)}) collective-permute-start(f32[64,128]{1,0:T(8,128)S(1)} %reduce_sum.117), channel_id=1, source_target_pairs={{0,1},{1,0},{2,3},{3,2},{4,5},{5,4},{6,7},{7,6},{8,9},{9,8},{10,11... | collective-permute-start | bytes 98312 | tf_op jit(solution)/shard_map/ppermute | solution.py:89
  97.7 23.2 %all-to-all-start.6 = ((f16[64,32,128]{2,1,0:T(8,128)(2,1)}), f16[64,32,128]{2,1,0:T(8,128)(2,1)S(1)}, u32[]{:S(2)}, u32[]{:S(2)}) async-start(f16[64,32,128]{2,1,0:T(8,128)(2,1)} %broadcast_in_dim.76), calls=%async_computation.6 | async-start | bytes 1048576 | tf_op jit(solution)/shard_map/all_to_all | solution.py:76
  129.3 14.6 %all-to-all-start.7 = ((f32[16,2,128]{2,1,0:T(2,128)}), f32[16,2,128]{2,1,0:T(2,128)S(1)}, u32[]{:S(2)}, u32[]{:S(2)}) async-start(f32[16,2,128]{2,1,0:T(2,128)} %broadcast_in_dim.77), calls=%async_computation.7 | async-start | bytes 32768 | tf_op jit(solution)/shard_map/all_to_all | solution.py:76
  221.9 15.1 %all-to-all-start.2 = ((f32[16,1,128]{2,1,0:T(1,128)}), f32[16,1,128]{2,1,0:T(1,128)S(1)}, u32[]{:S(2)}, u32[]{:S(2)}) async-start(f32[16,1,128]{2,1,0:T(1,128)} %broadcast_in_dim.9), calls=%async_computation.2 | async-start | bytes 16384 | tf_op jit(solution)/shard_map/cond/branch_0_fun/all_to_all | solution.py:76
  238.2 0.9 copy-start.1
  238.2 1.1 copy-start.3
  238.2 1.1 copy-start.4
